TPU v7x, 512 devices: a whole 4x4x16 slice. The times are simulated.
512 devices in a mesh: dp: 8 (over x, y_lo), tm: 64 (over z, y_hi, core).
Axes of the slice: x: 4, y: 4 (y_hi: 2, y_lo: 2; y = y_hi * 2 + y_lo), z: 16, core: 2. Of those that a mesh axis runs over, the one named last changes fastest.
Arguments:
- features: bfloat16 [8, 8192, 1536], P('dp', 'tm'), may hold values from -8 to 8
- start_noise: bfloat16 [8, 8192, 1536], P('dp', 'tm'), may hold values from -1 to 1
- cotangent: bfloat16 [8, 8192, 1536], P('dp', 'tm'), may hold values from -0.0234375 to 0.0234375
- in_weight: bfloat16 [3072, 1536], P('tm'), may hold values from -0.15625 to 0.15625
- kernel: float32 [31, 1536], replicated, may hold values from -1 to 1
- bn_gain: float32 [1536], replicated, may hold values from 0.25 to 1.75
- bn_shift: float32 [1536], replicated, may hold values from -1 to 1
- ends: int32 [8], replicated, may hold values from 4096 to 8192
Outputs:
- perturbation: float32 [8, 8192, 1536], P('dp', 'tm')
- grad_kernel: float32 [31, 1536], P(None, 'tm')
- grad_norm: float32 [2, 1536], P(None, 'tm')
Inputs may be any that keep to these rules, and one draw needn't show every extreme that they name: `ends`: frames at or after an utterance's end are padding.
All inputs are finite; a program needn't handle non-finite values.
Results may differ from a plain program's by a relative error of at most 0.0059.
Values may be sent and summed in bfloat16 or wider, within the bound.
A program may use at most 128 MiB of HBM per device.

v0:
```python
import jax
import jax.numpy as jnp
from jax import lax
from jax.sharding import PartitionSpec as P

ASCENT = 2


noise_scale = 0.5
ascent_rate = 0.5
layer_epsilon = 1e-05
batch_epsilon = 1e-05
ascent_epsilon = 1e-06


def normalize(summed):
    centre = summed - jnp.mean(summed, axis=-1, keepdims=True)
    inverse = lax.rsqrt(jnp.mean(centre * centre, axis=-1, keepdims=True) + layer_epsilon)
    return (centre * inverse, inverse)


def lane_conv_forward(padded, kernel, out_length):
    result = jnp.zeros((padded.shape[0], out_length), jnp.float32)
    for offset in range(kernel.shape[0]):
        result = result + kernel[offset][:, None] * padded[:, offset : offset + out_length].astype(
            jnp.float32
        )
    return result


def lane_conv_input_grad(padded, kernel, out_length):
    tap_span = kernel.shape[0] - 1
    result = jnp.zeros((padded.shape[0], out_length), jnp.float32)
    for offset in range(kernel.shape[0]):
        start_col = tap_span - offset
        result = result + kernel[offset][:, None] * padded[
            :, start_col : start_col + out_length
        ].astype(jnp.float32)
    return result


def lane_kernel_grad(grad_bf, padded, out_length):
    grad_float = grad_bf.astype(jnp.float32)
    rows_list = []
    for offset in range(padded.shape[1] - out_length + 1):
        rows_list.append(
            jnp.sum(
                grad_float * padded[:, offset : offset + out_length].astype(jnp.float32), axis=1
            )
        )
    return jnp.stack(rows_list)


def reduce_kernel(partial_grad):
    return lax.psum(partial_grad, "dp")


def on_device(features, start_noise, cotangent, in_weight, kernel, bn_gain, bn_shift, ends):
    frame_rows = features.shape[1]
    model_width = features.shape[2]
    tap_count = kernel.shape[0]
    half_span = (tap_count - 1) // 2
    shard_count = lax.axis_size("tm")
    shard_index = lax.axis_index("tm")
    group_index = lax.axis_index("dp")
    slice_width = model_width // shard_count
    all_frames = frame_rows * shard_count
    utter_end = lax.dynamic_index_in_dim(ends, group_index, 0, keepdims=False)
    live_count = jnp.sum(ends).astype(jnp.float32)
    utter_length = utter_end.astype(jnp.float32)
    frame_ids = shard_index * frame_rows + jnp.arange(frame_rows, dtype=jnp.int32)
    live_frames = (frame_ids < utter_end).astype(jnp.float32)
    live_whole = (jnp.arange(all_frames, dtype=jnp.int32) < utter_end).astype(jnp.float32)
    channel_start = shard_index * slice_width
    kernel_slice = lax.dynamic_slice_in_dim(kernel, channel_start, slice_width, 1)
    gain_slice = lax.dynamic_slice_in_dim(bn_gain, channel_start, slice_width, 0)
    shift_slice = lax.dynamic_slice_in_dim(bn_shift, channel_start, slice_width, 0)
    weight_full = lax.all_gather(in_weight, "tm", axis=0, tiled=True)
    inputs = features[0].astype(jnp.float32)
    perturbation = noise_scale * start_noise[0].astype(jnp.float32) * live_frames[:, None]
    cot_channels = lax.all_to_all(
        jnp.transpose(cotangent[0])[None], "tm", split_axis=1, concat_axis=2, tiled=True
    )[0]
    upstream = live_whole[None, :] * cot_channels.astype(jnp.float32) / ASCENT
    kernel_total = jnp.zeros((tap_count, slice_width), jnp.float32)
    norm_total = jnp.zeros((2, slice_width), jnp.float32)
    for ascent_step in range(ASCENT):
        summed = inputs + perturbation
        normed, inverse = normalize(summed)
        hidden = lax.dot_general(
            normed.astype(jnp.bfloat16),
            weight_full,
            (((1,), (1,)), ((), ())),
            preferred_element_type=jnp.float32,
        )
        value_half = hidden[:, :model_width]
        gate_half = jax.nn.sigmoid(hidden[:, model_width:])
        glu = (value_half * gate_half * live_frames[:, None]).astype(jnp.bfloat16)
        glu_local = lax.all_to_all(
            jnp.transpose(glu)[None], "tm", split_axis=1, concat_axis=2, tiled=True
        )[0]
        padded = jnp.pad(glu_local, ((0, 0), (half_span, half_span)))
        conv_out = lane_conv_forward(padded, kernel_slice, all_frames)
        live_mask = live_whole[None, :]
        batch_mean = lax.psum(jnp.sum(live_mask * conv_out, axis=1), "dp") / live_count
        centred = conv_out - batch_mean[:, None]
        variance = lax.psum(jnp.sum(live_mask * centred * centred, axis=1), "dp") / live_count
        inv_std = lax.rsqrt(variance + batch_epsilon)[:, None]
        gain_now, shift_now = (gain_slice[:, None], shift_slice[:, None])
        scaled = centred * inv_std
        pre_act = gain_now * scaled + shift_now
        pre_sigmoid = jax.nn.sigmoid(pre_act)
        grad_pre = upstream * pre_sigmoid * (1.0 + pre_act * (1.0 - pre_sigmoid))
        shift_sum, gain_sum = lax.psum(
            (jnp.sum(grad_pre, axis=1), jnp.sum(grad_pre * scaled, axis=1)), "dp"
        )
        norm_total = norm_total + jnp.stack([gain_sum, shift_sum])
        grad_conv = (
            live_mask
            * inv_std
            * gain_now
            * (grad_pre - (shift_sum[:, None] + scaled * gain_sum[:, None]) / live_count)
        ).astype(jnp.bfloat16)
        kernel_part = lane_kernel_grad(grad_conv, padded, all_frames)
        kernel_total = kernel_total + reduce_kernel(kernel_part)
        if ascent_step + 1 < ASCENT:
            grad_pad = jnp.pad(grad_conv, ((0, 0), (half_span, half_span)))
            grad_local = (
                lane_conv_input_grad(grad_pad, kernel_slice, all_frames) * live_mask
            ).astype(jnp.bfloat16)
            grad_glu = jnp.transpose(
                lax.all_to_all(grad_local[None], "tm", split_axis=2, concat_axis=1, tiled=True)[0]
            )
            grad_float = grad_glu.astype(jnp.float32)
            grad_hidden = jnp.concatenate(
                [grad_float * gate_half, grad_float * value_half * gate_half * (1.0 - gate_half)],
                axis=1,
            ).astype(jnp.bfloat16)
            grad_normed = jnp.dot(grad_hidden, weight_full, preferred_element_type=jnp.float32)
            grad_sum = inverse * (
                grad_normed
                - jnp.mean(grad_normed, axis=-1, keepdims=True)
                - normed * jnp.mean(grad_normed * normed, axis=-1, keepdims=True)
            )
            direction = live_frames[:, None] * grad_sum
            square_total = lax.psum(jnp.sum(direction * direction), "tm")
            perturbation = perturbation + direction * (
                ascent_rate
                * jnp.sqrt(utter_length * model_width)
                / (jnp.sqrt(square_total) + ascent_epsilon)
            )
    return (perturbation[None], kernel_total, norm_total)


def solution(mesh):
    return jax.shard_map(
        on_device,
        mesh=mesh,
        in_specs=(
            P("dp", "tm", None),
            P("dp", "tm", None),
            P("dp", "tm", None),
            P("tm", None),
            P(),
            P(),
            P(),
            P(),
        ),
        out_specs=(P("dp", "tm", None), P(None, "tm"), P(None, "tm")),
        check_vma=False,
    )
```

profile of v0, /device:TPU:16, one launch (start us, length us, event | category | flops | bytes accessed | tf_op | source)
XLA Modules:
  0.0 742.7 jit_solution(14522599243444606599)
XLA Ops:
  15.8 8.8 %reduce.1 = bf16[1536,128]{1,0:T(8,128)(2,1)S(1)} reduce(bf16[1536,1,128]{2,1,0:T(2,128)(2,1)S(1)} %bitcast.268, bf16[]{:T(256)} %broadcast.129), dimensions={1}, to_apply=%bitcast.247.reduce_sub_computation | reduce | bytes 786434
  25.5 19.2 %all-to-all-start.1 = ((bf16[64,2,1536]{2,1,0:T(2,128)(2,1)}), bf16[64,2,1536]{2,1,0:T(2,128)(2,1)S(1)}, u32[]{:S(2)}, u32[]{:S(2)}) async-start(bf16[64,2,1536]{2,1,0:T(2,128)(2,1)} %reshape.112), calls=%async_computation.1 | async-start | bytes 786432 | tf_op jit(solution)/shard_map/all_to_all | solution.py:81
  47.3 139.9 %all-gather.2.cloned.1.call-done = bf16[3072,1536]{1,0:T(8,128)(2,1)} async-done(((bf16[48,1536]{1,0:T(8,128)(2,1)}), bf16[3072,1536]{1,0:T(8,128)(2,1)}) %all-gather.2.cloned.1.call-update) | async-done | bytes 9437200 | tf_op jit(solution)/shard_map/all_gather | solution.py:78
  187.3 6.9 fusion.162
  197.4 9.5 %reduce = bf16[1536,128]{1,0:T(8,128)(2,1)} reduce(bf16[1536,1,128]{2,1,0:T(2,128)(2,1)S(1)} %bitcast.270, bf16[]{:T(256)} %broadcast.129), dimensions={1}, to_apply=%bitcast.227.reduce_sub_computation | reduce | bytes 786434
  208.7 11.1 %all-to-all-start = ((bf16[64,2,1536]{2,1,0:T(2,128)(2,1)}), bf16[64,2,1536]{2,1,0:T(2,128)(2,1)}, u32[]{:S(2)}, u32[]{:S(2)}) async-start(bf16[64,2,1536]{2,1,0:T(2,128)(2,1)} %reshape.114), calls=%async_computation | async-start | bytes 786432 | tf_op jit(solution)/shard_map/all_to_all | solution.py:99
  230.4 17.4 %all-to-all-done = bf16[64,2,1536]{2,1,0:T(2,128)(2,1)} async-done(((bf16[64,2,1536]{2,1,0:T(2,128)(2,1)}), bf16[64,2,1536]{2,1,0:T(2,128)(2,1)}, u32[]{:S(2)}, u32[]{:S(2)}) %all-to-all-start) | async-done | bytes 393248 | tf_op jit(solution)/shard_map/all_to_all | solution.py:99
  257.4 20.7 %psum.77 = f32[24]{0:T(128)} all-reduce(f32[24]{0:T(128)} %get-tuple-element.100), channel_id=1, replica_groups=mesh['dp'=8,'tm'=64] {'dp'}, use_global_device_ids=true, to_apply=%region_3.4 | all-reduce | flops 24 | bytes 192 | tf_op jit(solution)/shard_map/psum | solution.py:105
  280.9 16.6 %psum.78 = f32[24]{0:T(128)} all-reduce(f32[24]{0:T(128)} %fusion.60), channel_id=1, replica_groups=mesh['dp'=8,'tm'=64] {'dp'}, use_global_device_ids=true, to_apply=%region_6.7 | all-reduce | flops 24 | bytes 192 | tf_op jit(solution)/shard_map/psum | solution.py:107
  302.1 18.8 %all-reduce.4 = (f32[24]{0:T(128)}, f32[24]{0:T(128)}) all-reduce(f32[24]{0:T(128)} %get-tuple-element.83, f32[24]{0:T(128)} %get-tuple-element.82), channel_id=1, replica_groups=mesh['dp'=8,'tm'=64] {'dp'}, use_global_device_ids=true, to_apply=%region_10.11 | all-reduce | flops 48 | bytes 384 | tf_op jit(solution)/shard_map/psum | solution.py:114
  330.3 6.7 copy.52
  337.0 46.5 %reduce.2 = bf16[8192,24]{1,0:T(8,128)(2,1)} reduce(bf16[8192,1,24]{2,1,0:T(2,128)(2,1)} %bitcast.248, bf16[]{:T(256)} %broadcast.129), dimensions={1}, to_apply=%bitcast.229.reduce_sub_computation | reduce | bytes 786434
  394.8 27.1 %all-to-all-done.2 = bf16[64,2,1536]{2,1,0:T(2,128)(2,1)S(1)} async-done(((bf16[64,2,1536]{2,1,0:T(2,128)(2,1)}), bf16[64,2,1536]{2,1,0:T(2,128)(2,1)S(1)}, u32[]{:S(2)}, u32[]{:S(2)}) %all-to-all-start.2) | async-done | bytes 393248 | tf_op jit(solution)/shard_map/all_to_all | solution.py:132
  421.9 8.9 %reshape.117 = bf16[8192,1,24]{2,1,0:T(2,128)(2,1)} reshape(bf16[64,2,1536]{2,1,0:T(2,128)(2,1)S(1)} %all-to-all-done.2) | data formatting | bytes 786432
  430.8 8.0 %copy.53 = bf16[1,24,8192]{2,1,0:T(8,128)(2,1)S(1)} copy(bf16[1,24,8192]{1,0,2:T(2,128)(2,1)} %bitcast.249) | data formatting | bytes 786432 | tf_op jit(solution)/shard_map/all_to_all | solution.py:132
  448.7 125.4 %psum.81 = f32[]{:T(128)} all-reduce(f32[]{:T(128)} %get-tuple-element.97), channel_id=1, replica_groups=mesh['dp'=8,'tm'=64] {'tm'}, use_global_device_ids=true, to_apply=%region_14.15 | all-reduce | flops 1 | bytes 8 | tf_op jit(solution)/shard_map/psum | solution.py:146
  576.2 6.8 fusion.165
  583.8 8.8 %reduce.3 = bf16[1536,128]{1,0:T(8,128)(2,1)S(1)} reduce(bf16[1536,1,128]{2,1,0:T(2,128)(2,1)S(1)} %bitcast.269, bf16[]{:T(256)} %broadcast.129), dimensions={1}, to_apply=%bitcast.231.reduce_sub_computation | reduce | bytes 786434
  593.4 11.4 %all-to-all-start.3 = ((bf16[64,2,1536]{2,1,0:T(2,128)(2,1)}), bf16[64,2,1536]{2,1,0:T(2,128)(2,1)S(1)}, u32[]{:S(2)}, u32[]{:S(2)}) async-start(bf16[64,2,1536]{2,1,0:T(2,128)(2,1)} %reshape.118), calls=%async_computation.3 | async-start | bytes 786432 | tf_op jit(solution)/shard_map/all_to_all | solution.py:99
  608.7 24.0 %all-to-all-done.3 = bf16[64,2,1536]{2,1,0:T(2,128)(2,1)S(1)} async-done(((bf16[64,2,1536]{2,1,0:T(2,128)(2,1)}), bf16[64,2,1536]{2,1,0:T(2,128)(2,1)S(1)}, u32[]{:S(2)}, u32[]{:S(2)}) %all-to-all-start.3) | async-done | bytes 393248 | tf_op jit(solution)/shard_map/all_to_all | solution.py:99
  639.5 16.1 %psum.83 = f32[24]{0:T(128)S(1)} all-reduce(f32[24]{0:T(128)} %get-tuple-element.92), channel_id=1, replica_groups=mesh['dp'=8,'tm'=64] {'dp'}, use_global_device_ids=true, to_apply=%region_50.51 | all-reduce | flops 24 | bytes 192 | tf_op jit(solution)/shard_map/psum | solution.py:105
  656.6 18.0 %psum.84 = f32[24]{0:T(128)S(1)} all-reduce(f32[24]{0:T(128)S(1)} %fusion.61), channel_id=1, replica_groups=mesh['dp'=8,'tm'=64] {'dp'}, use_global_device_ids=true, to_apply=%region_52.53 | all-reduce | flops 24 | bytes 192 | tf_op jit(solution)/shard_map/psum | solution.py:107
  677.8 16.4 %all-reduce.3 = (f32[24]{0:T(128)S(1)}, f32[24]{0:T(128)S(1)}) all-reduce(f32[24]{0:T(128)} %get-tuple-element.49, f32[24]{0:T(128)} %get-tuple-element.48), channel_id=1, replica_groups=mesh['dp'=8,'tm'=64] {'dp'}, use_global_device_ids=true, to_apply=%region_56.57 | all-reduce | flops 48 | bytes 384 | tf_op jit(solution)/shard_map/psum | solution.py:114
  701.7 32.5 %psum.88 = f32[31,24]{1,0:T(8,128)S(1)} all-reduce(f32[31,24]{1,0:T(8,128)S(1)} %add.520), channel_id=1, replica_groups=mesh['dp'=8,'tm'=64] {'dp'}, use_global_device_ids=true, to_apply=%region_46.47 | all-reduce | flops 744 | bytes 5952 | tf_op jit(solution)/shard_map/psum | solution.py:55
  (170 shorter events, 99.7 us)
Async XLA Ops:
  7.2 37.6 %copy-start.46 = (s32[8]{0:T(128)S(1)}, s32[8]{0:T(128)}, u32[]{:S(2)}) copy-start(s32[8]{0:T(128)} %param.15) | copy-start | bytes 100
  7.2 38.8 %copy-start.1 = (bf16[1,128,1536]{2,1,0:T(8,128)(2,1)S(1)}, bf16[1,128,1536]{2,1,0:T(8,128)(2,1)}, u32[]{:S(2)}) copy-start(bf16[1,128,1536]{2,1,0:T(8,128)(2,1)} %param.8) | copy-start | bytes 1179652
  7.2 38.8 %copy-start = (bf16[1,128,1536]{2,1,0:T(8,128)(2,1)S(1)}, bf16[1,128,1536]{2,1,0:T(8,128)(2,1)}, u32[]{:S(2)}) copy-start(bf16[1,128,1536]{2,1,0:T(8,128)(2,1)} %param.9) | copy-start | bytes 1179652
  7.2 180.1 %all-gather.2.cloned.1.call-start = ((), (), s32[]{:S(2)}) async-start(), calls=%async_computation.4 | async-start | bytes 9584640 | tf_op jit(solution)/shard_map/all_gather | solution.py:78
  25.5 183.2 %all-to-all-start.1 = ((bf16[64,2,1536]{2,1,0:T(2,128)(2,1)}), bf16[64,2,1536]{2,1,0:T(2,128)(2,1)S(1)}, u32[]{:S(2)}, u32[]{:S(2)}) async-start(bf16[64,2,1536]{2,1,0:T(2,128)(2,1)} %reshape.112), calls=%async_computation.1 | async-start | bytes 786432 | tf_op jit(solution)/shard_map/all_to_all | solution.py:81
  46.3 147.9 %copy-start.11 = (f32[128]{0:T(128)}, f32[128]{0:T(128)S(1)}, u32[]{:S(2)}) copy-start(f32[128]{0:T(128)S(1)} %broadcast_multiply_fusion.3) | copy-start | bytes 1540
  47.0 147.2 %copy-start.8 = (f32[128]{0:T(128)}, f32[128]{0:T(128)S(1)}, u32[]{:S(2)}) copy-start(f32[128]{0:T(128)S(1)} %compare_convert_fusion) | copy-start | bytes 1540
  47.3 146.9 %copy-start.40 = (f32[128]{0:T(128)}, f32[128]{0:T(128)S(1)}, u32[]{:S(2)}) copy-start(f32[128]{0:T(128)S(1)} %add_rsqrt_fusion.3) | copy-start | bytes 1540
  208.7 39.0 %all-to-all-start = ((bf16[64,2,1536]{2,1,0:T(2,128)(2,1)}), bf16[64,2,1536]{2,1,0:T(2,128)(2,1)}, u32[]{:S(2)}, u32[]{:S(2)}) async-start(bf16[64,2,1536]{2,1,0:T(2,128)(2,1)} %reshape.114), calls=%async_computation | async-start | bytes 786432 | tf_op jit(solution)/shard_map/all_to_all | solution.py:99
  388.3 33.6 %all-to-all-start.2 = ((bf16[64,2,1536]{2,1,0:T(2,128)(2,1)}), bf16[64,2,1536]{2,1,0:T(2,128)(2,1)S(1)}, u32[]{:S(2)}, u32[]{:S(2)}) async-start(bf16[64,2,1536]{2,1,0:T(2,128)(2,1)} %reshape.116), calls=%async_computation.2 | async-start | bytes 786432 | tf_op jit(solution)/shard_map/all_to_all | solution.py:132
  583.8 49.7 %copy-start.7 = (f32[24]{0:T(128)S(1)}, f32[24]{0:T(128)}, u32[]{:S(2)}) copy-start(f32[24]{0:T(128)} %get-tuple-element.108) | copy-start | bytes 292
  593.4 81.1 %copy-start.4 = (f32[1,24,64,128]{3,2,1,0:T(8,128)S(1)}, f32[1,24,64,128]{3,2,1,0:T(8,128)}, u32[]{:S(2)}) copy-start(f32[1,24,64,128]{3,2,1,0:T(8,128)} %copy.51) | copy-start | bytes 2359300
  593.4 39.3 %all-to-all-start.3 = ((bf16[64,2,1536]{2,1,0:T(2,128)(2,1)}), bf16[64,2,1536]{2,1,0:T(2,128)(2,1)S(1)}, u32[]{:S(2)}, u32[]{:S(2)}) async-start(bf16[64,2,1536]{2,1,0:T(2,128)(2,1)} %reshape.118), calls=%async_computation.3 | async-start | bytes 786432 | tf_op jit(solution)/shard_map/all_to_all | solution.py:99
  633.5 66.3 %copy-start.6 = (bf16[1,24,64,128]{3,2,1,0:T(8,128)(2,1)S(1)}, bf16[1,24,64,128]{3,2,1,0:T(8,128)(2,1)}, u32[]{:S(2)}) copy-start(bf16[1,24,64,128]{3,2,1,0:T(8,128)(2,1)} %copy-done.5) | copy-start | bytes 1179652
  674.6 26.7 %copy-start.13 = (f32[24]{0:T(128)S(1)}, f32[24]{0:T(128)}, u32[]{:S(2)}) copy-start(f32[24]{0:T(128)} %get-tuple-element.50) | copy-start | bytes 292
  674.6 26.7 %copy-start.14 = (f32[24]{0:T(128)S(1)}, f32[24]{0:T(128)}, u32[]{:S(2)}) copy-start(f32[24]{0:T(128)} %get-tuple-element.51) | copy-start | bytes 292
  674.6 26.7 %copy-start.15 = (f32[24]{0:T(128)S(1)}, f32[24]{0:T(128)}, u32[]{:S(2)}) copy-start(f32[24]{0:T(128)} %get-tuple-element.52) | copy-start | bytes 292
  677.6 23.8 %copy-start.19 = (f32[24]{0:T(128)S(1)}, f32[24]{0:T(128)}, u32[]{:S(2)}) copy-start(f32[24]{0:T(128)} %get-tuple-element.56) | copy-start | bytes 292
  677.6 23.8 %copy-start.20 = (f32[24]{0:T(128)S(1)}, f32[24]{0:T(128)}, u32[]{:S(2)}) copy-start(f32[24]{0:T(128)} %get-tuple-element.57) | copy-start | bytes 292
  677.6 23.8 %copy-start.21 = (f32[24]{0:T(128)S(1)}, f32[24]{0:T(128)}, u32[]{:S(2)}) copy-start(f32[24]{0:T(128)} %get-tuple-element.58) | copy-start | bytes 292
  677.6 23.8 %copy-start.22 = (f32[24]{0:T(128)S(1)}, f32[24]{0:T(128)}, u32[]{:S(2)}) copy-start(f32[24]{0:T(128)} %get-tuple-element.59) | copy-start | bytes 292
  677.6 23.8 %copy-start.23 = (f32[24]{0:T(128)S(1)}, f32[24]{0:T(128)}, u32[]{:S(2)}) copy-start(f32[24]{0:T(128)} %get-tuple-element.60) | copy-start | bytes 292
  677.8 57.0 %copy-start.44 = (f32[24]{0:T(128)S(1)}, f32[24]{0:T(128)}, u32[]{:S(2)}) copy-start(f32[24]{0:T(128)} %get-tuple-element.88) | copy-start | bytes 292
  677.8 57.0 %copy-start.45 = (f32[24]{0:T(128)S(1)}, f32[24]{0:T(128)}, u32[]{:S(2)}) copy-start(f32[24]{0:T(128)} %get-tuple-element.89) | copy-start | bytes 292
  (28 other events, 495.2 us)
Sparse Core Ops, SparseCore 0:
  11.3 175.9 all-gather.1
where the time goes:
time: 750 us; the launch traced here: 743 us
  blocking collectives  264 us (35%)
  waiting for transfers between devices  209 us (28%)
  other arithmetic  125 us (17%)
  local copies, waits for them, and re-layouts  60.1 us (8%)
  starting transfers between devices  47.6 us (6%)
  matrix products  19 us (3%)
  between operations  17.5 us (2%)
    all_gather x1, waiting for transfers between devices, on_device(): weight_full = lax.all_gather(in_weight, 'tm', axis=0, tiled=True)  140 us
    psum x1, blocking collectives, on_device(): square_total = lax.psum(jnp.sum(direction * direction), 'tm')  125 us
    unnamed x5, other arithmetic  73.6 us
    all_to_all x2, waiting for transfers between devices, on_device(): lax.all_to_all(jnp.transpose(glu)[None], 'tm', split_axis=1, concat_axis=...  41.4 us
    psum x2, blocking collectives, on_device(): lax.psum(jnp.sum(live_mask * conv_out, axis=1), 'dp') / live_count  36.8 us
    psum x2, blocking collectives, on_device(): lax.psum((jnp.sum(grad_pre, axis=1), jnp.sum(grad_pre * scaled, axis=1)),...  35.2 us
    psum x2, blocking collectives, on_device(): lax.psum(jnp.sum(live_mask * centred * centred, axis=1), 'dp') / live_count  34.5 us
    psum x1, blocking collectives, reduce_kernel(): return lax.psum(partial_grad, 'dp')  32.5 us
  transfers between devices with their start and end apart: 5, of which 4 were waited for; matrix products, arithmetic and copies ran while one was open for 7% of the time, Pallas kernels for 0%

commit v1 on v0

v1 whole, which is shorter than its diff:
```python
import jax
import jax.numpy as jnp
from jax import lax
from jax.sharding import PartitionSpec as P

ASCENT = 2

noise_scale = 0.5
ascent_rate = 0.5
layer_epsilon = 1e-05
batch_epsilon = 1e-05
ascent_epsilon = 1e-06


def normalize(summed):
    centre = summed - jnp.mean(summed, axis=-1, keepdims=True)
    inverse = lax.rsqrt(jnp.mean(centre * centre, axis=-1, keepdims=True) + layer_epsilon)
    return (centre * inverse, inverse)


def with_halo(block, half_span):
    count = lax.axis_size("tm")
    before = lax.ppermute(block[-half_span:], "tm", [(i, i + 1) for i in range(count - 1)])
    after = lax.ppermute(block[:half_span], "tm", [(i + 1, i) for i in range(count - 1)])
    return jnp.concatenate([before, block, after], axis=0).astype(jnp.float32)


def conv(padded, kernel, out_length, flip):
    taps = kernel.shape[0]
    result = None
    for offset in range(taps):
        start = taps - 1 - offset if flip else offset
        term = kernel[offset] * padded[start : start + out_length]
        result = term if result is None else result + term
    return result


def tap_grad(grad, padded, taps):
    rows = grad.shape[0]
    return jnp.stack([jnp.sum(grad * padded[j : j + rows], axis=0) for j in range(taps)])


def on_device(features, start_noise, cotangent, in_weight, kernel, bn_gain, bn_shift, ends):
    frame_rows = features.shape[1]
    model_width = features.shape[2]
    tap_count = kernel.shape[0]
    half_span = (tap_count - 1) // 2
    shard_index = lax.axis_index("tm")
    group_index = lax.axis_index("dp")
    utter_end = lax.dynamic_index_in_dim(ends, group_index, 0, keepdims=False)
    live_count = jnp.sum(ends).astype(jnp.float32)
    utter_length = utter_end.astype(jnp.float32)
    frame_ids = shard_index * frame_rows + jnp.arange(frame_rows, dtype=jnp.int32)
    live = (frame_ids < utter_end).astype(jnp.float32)[:, None]
    weight_full = lax.all_gather(in_weight, "tm", axis=0, tiled=True)
    inputs = features[0].astype(jnp.float32)
    perturbation = noise_scale * start_noise[0].astype(jnp.float32) * live
    upstream = live * cotangent[0].astype(jnp.float32) / ASCENT
    everywhere = ("dp", "tm")
    kernel_part = 0.0
    norm_part = 0.0
    for ascent_step in range(ASCENT):
        summed = inputs + perturbation
        normed, inverse = normalize(summed)
        hidden = lax.dot_general(
            normed.astype(jnp.bfloat16),
            weight_full,
            (((1,), (1,)), ((), ())),
            preferred_element_type=jnp.float32,
        )
        value_half = hidden[:, :model_width]
        gate_half = jax.nn.sigmoid(hidden[:, model_width:])
        glu = (value_half * gate_half * live).astype(jnp.bfloat16)
        padded = with_halo(glu, half_span)
        conv_out = conv(padded, kernel, frame_rows, False)
        batch_mean = lax.psum(jnp.sum(live * conv_out, axis=0), everywhere) / live_count
        centred = conv_out - batch_mean
        variance = lax.psum(jnp.sum(live * centred * centred, axis=0), everywhere) / live_count
        inv_std = lax.rsqrt(variance + batch_epsilon)
        scaled = centred * inv_std
        pre_act = bn_gain * scaled + bn_shift
        pre_sigmoid = jax.nn.sigmoid(pre_act)
        grad_pre = upstream * pre_sigmoid * (1.0 + pre_act * (1.0 - pre_sigmoid))
        both = lax.psum(
            jnp.stack([jnp.sum(grad_pre * scaled, axis=0), jnp.sum(grad_pre, axis=0)]), everywhere
        )
        norm_part = norm_part + both
        grad_conv = (
            live * inv_std * bn_gain * (grad_pre - (both[1] + scaled * both[0]) / live_count)
        ).astype(jnp.bfloat16)
        kernel_part = kernel_part + tap_grad(grad_conv.astype(jnp.float32), padded, tap_count)
        if ascent_step + 1 < ASCENT:
            grad_pad = with_halo(grad_conv, half_span)
            grad_glu = (conv(grad_pad, kernel, frame_rows, True) * live).astype(jnp.bfloat16)
            grad_float = grad_glu.astype(jnp.float32)
            grad_hidden = jnp.concatenate(
                [grad_float * gate_half, grad_float * value_half * gate_half * (1.0 - gate_half)],
                axis=1,
            ).astype(jnp.bfloat16)
            grad_normed = jnp.dot(grad_hidden, weight_full, preferred_element_type=jnp.float32)
            direction = (
                live
                * inverse
                * (
                    grad_normed
                    - jnp.mean(grad_normed, axis=-1, keepdims=True)
                    - normed * jnp.mean(grad_normed * normed, axis=-1, keepdims=True)
                )
            )
            square_total = lax.psum(jnp.sum(direction * direction), "tm")
            perturbation = perturbation + direction * (
                ascent_rate
                * jnp.sqrt(utter_length * model_width)
                / (jnp.sqrt(square_total) + ascent_epsilon)
            )
    width = model_width // lax.axis_size("tm")
    by_shard = jnp.transpose(kernel_part.reshape(tap_count, -1, width), (1, 0, 2))
    by_shard = jnp.pad(by_shard.reshape(by_shard.shape[0], -1), ((0, 0), (0, 24)))
    kernel_total = lax.psum_scatter(by_shard.reshape(-1, 6, 128), "tm", scatter_dimension=0)
    kernel_total = lax.psum(kernel_total, "dp").reshape(-1)[: tap_count * width]
    kernel_total = kernel_total.reshape(tap_count, width)
    norm_total = lax.dynamic_slice_in_dim(norm_part, shard_index * width, width, 1)
    return (perturbation[None], kernel_total, norm_total)


def solution(mesh):
    return jax.shard_map(
        on_device,
        mesh=mesh,
        in_specs=(
            P("dp", "tm", None),
            P("dp", "tm", None),
            P("dp", "tm", None),
            P("tm", None),
            P(),
            P(),
            P(),
            P(),
        ),
        out_specs=(P("dp", "tm", None), P(None, "tm"), P(None, "tm")),
        check_vma=False,
    )
```

time: 750 us -> 1540 us (2.05)
  the two profiles are of different devices: /device:TPU:16 before, /device:TPU:1 now
where the time goes in v1:
time: 1540 us; the launch traced here: 1530 us
  blocking collectives  767 us (50%)
  waiting for transfers between devices  654 us (42%)
  other arithmetic  38 us (2%)
  local copies, waits for them, and re-layouts  21.8 us (1%)
  starting transfers between devices  18.7 us (1%)
  between operations  17.9 us (1%)
    unnamed x3, waiting for transfers between devices  476 us
    psum x2, blocking collectives, on_device(): lax.psum(jnp.sum(live * conv_out, axis=0), everywhere) / live_count  217 us
    psum x2, blocking collectives, on_device(): lax.psum(jnp.stack([jnp.sum(grad_pre * scaled, axis=0), jnp.sum(grad_pre,...  201 us
    psum x2, blocking collectives, on_device(): lax.psum(jnp.sum(live * centred * centred, axis=0), everywhere) / live_count  198 us
    all_gather x1, waiting for transfers between devices, on_device(): weight_full = lax.all_gather(in_weight, 'tm', axis=0, tiled=True)  170 us
    psum x1, blocking collectives, on_device(): square_total = lax.psum(jnp.sum(direction * direction), 'tm')  125 us
  transfers between devices with their start and end apart: 8, of which 5 were waited for; matrix products, arithmetic and copies ran while one was open for 1% of the time, Pallas kernels for 0%

profile of v1, /device:TPU:1, one launch (start us, length us, event | category | flops | bytes accessed | tf_op | source)
XLA Modules:
  0.0 1532.0 jit_solution(2124826723035073364)
XLA Ops:
  16.3 169.8 %all-gather.2.cloned.1.call-done = bf16[3072,1536]{1,0:T(8,128)(2,1)} async-done(((bf16[48,1536]{1,0:T(8,128)(2,1)}), bf16[3072,1536]{1,0:T(8,128)(2,1)}) %all-gather.2.cloned.1.call-update) | async-done | bytes 9437200 | tf_op jit(solution)/shard_map/all_gather | solution.py:55
  186.2 6.9 fusion.122
  193.4 2.3 collective-permute-start
  202.8 4.6 multiply_reduce_fusion.6
  207.3 104.6 %psum.56 = f32[1536]{0:T(1024)} all-reduce(f32[1536]{0:T(1024)} %get-tuple-element.124), channel_id=1, replica_groups=mesh['dp'=8,'tm'=64] {'dp','tm'}, use_global_device_ids=true, to_apply=%region_3.4 | all-reduce | flops 1536 | bytes 12288 | tf_op jit(solution)/shard_map/psum | solution.py:76
  314.1 98.7 %psum.57 = f32[1536]{0:T(1024)} all-reduce(f32[1536]{0:T(1024)} %fusion.4), channel_id=1, replica_groups=mesh['dp'=8,'tm'=64] {'dp','tm'}, use_global_device_ids=true, to_apply=%region_6.7 | all-reduce | flops 1536 | bytes 12288 | tf_op jit(solution)/shard_map/psum | solution.py:78
  414.0 2.4 multiply_reduce_fusion.5
  417.0 100.3 %psum.58 = f32[2,1536]{1,0:T(2,128)} all-reduce(f32[2,1536]{1,0:T(2,128)} %pad_maximum_fusion), channel_id=1, replica_groups=mesh['dp'=8,'tm'=64] {'dp','tm'}, use_global_device_ids=true, to_apply=%region_9.10 | all-reduce | flops 3072 | bytes 24576 | tf_op jit(solution)/shard_map/psum | solution.py:84
  518.2 4.1 fusion.36
  528.6 4.0 collective-permute-start.2
  535.1 4.5 collective-permute-done.3
  539.8 3.2 fusion
  546.9 124.9 %psum.59 = f32[]{:T(128)} all-reduce(f32[]{:T(128)} %get-tuple-element.119), channel_id=1, replica_groups=mesh['dp'=8,'tm'=64] {'tm'}, use_global_device_ids=true, to_apply=%region_13.14 | all-reduce | flops 1 | bytes 8 | tf_op jit(solution)/shard_map/psum | solution.py:110
  674.0 6.8 fusion.124
  681.1 4.1 collective-permute-start.4
  685.2 4.2 collective-permute-start.5
  689.5 2.6 collective-permute-done.5
  692.3 3.1 multiply_reduce_fusion.1
  695.5 112.3 %psum.60 = f32[1536]{0:T(1024)S(1)} all-reduce(f32[1536]{0:T(1024)S(1)} %get-tuple-element.114), channel_id=1, replica_groups=mesh['dp'=8,'tm'=64] {'dp','tm'}, use_global_device_ids=true, to_apply=%region_48.49 | all-reduce | flops 1536 | bytes 12288 | tf_op jit(solution)/shard_map/psum | solution.py:76
  808.0 99.3 %psum.61 = f32[1536]{0:T(1024)S(1)} all-reduce(f32[1536]{0:T(1024)S(1)} %fusion.5), channel_id=1, replica_groups=mesh['dp'=8,'tm'=64] {'dp','tm'}, use_global_device_ids=true, to_apply=%region_50.51 | all-reduce | flops 1536 | bytes 12288 | tf_op jit(solution)/shard_map/psum | solution.py:78
  908.6 100.5 %psum.62 = f32[2,1536]{1,0:T(2,128)S(1)} all-reduce(f32[2,1536]{1,0:T(2,128)S(1)} %pad_maximum_fusion.1), channel_id=1, replica_groups=mesh['dp'=8,'tm'=64] {'dp','tm'}, use_global_device_ids=true, to_apply=%region_53.54 | all-reduce | flops 3072 | bytes 24576 | tf_op jit(solution)/shard_map/psum | solution.py:84
  1009.1 2.3 fusion.67
  1021.7 475.0 %all-reduce.4.cloned.1.call-done = f32[64,6,128]{2,1,0:T(8,128)} async-done(((f32[64,6,128]{2,1,0:T(8,128)}), f32[64,6,128]{2,1,0:T(8,128)}) %all-reduce.4.cloned.1.call-update) | async-done | bytes 196624
  1498.2 26.2 %psum.63 = f32[32,24]{1,0:T(8,128)S(1)} all-reduce(f32[32,24]{1,0:T(8,128)S(1)} %slice.682), channel_id=1, replica_groups=mesh['dp'=8,'tm'=64] {'dp'}, use_global_device_ids=true, to_apply=%region_86.87 | all-reduce | flops 768 | bytes 6144 | tf_op jit(solution)/shard_map/psum | solution.py:120
  (354 shorter events, 47.2 us)
Async XLA Ops:
  7.2 179.0 %copy-start = (bf16[1,128,1536]{2,1,0:T(8,128)(2,1)S(1)}, bf16[1,128,1536]{2,1,0:T(8,128)(2,1)}, u32[]{:S(2)}) copy-start(bf16[1,128,1536]{2,1,0:T(8,128)(2,1)} %param.9) | copy-start | bytes 1179652
  7.2 179.0 %copy-start.2 = (bf16[1,128,1536]{2,1,0:T(8,128)(2,1)S(1)}, bf16[1,128,1536]{2,1,0:T(8,128)(2,1)}, u32[]{:S(2)}) copy-start(bf16[1,128,1536]{2,1,0:T(8,128)(2,1)} %param.8) | copy-start | bytes 1179652
  7.2 179.0 %all-gather.2.cloned.1.call-start = ((), (), s32[]{:S(2)}) async-start(), calls=%async_computation | async-start | bytes 9584640 | tf_op jit(solution)/shard_map/all_gather | solution.py:55
  7.9 1488.8 %all-reduce.4.cloned.1.call-start = ((), (), s32[]{:S(2)}) async-start(), calls=%async_computation.1 | async-start | bytes 524288
  9.9 183.2 %copy-start.22 = (f32[128]{0:T(128)}, f32[128]{0:T(128)S(1)}, u32[]{:S(2)}) copy-start(f32[128]{0:T(128)S(1)} %fusion.133) | copy-start | bytes 1540
  10.5 182.6 %copy-start.42 = (f32[128]{0:T(128)}, f32[128]{0:T(128)S(1)}, u32[]{:S(2)}) copy-start(f32[128]{0:T(128)S(1)} %broadcast_select_fusion.1) | copy-start | bytes 1540
  13.7 179.5 %copy-start.46 = (f32[128]{0:T(128)}, f32[128]{0:T(128)S(1)}, u32[]{:S(2)}) copy-start(f32[128]{0:T(128)S(1)} %broadcast_multiply_fusion.3) | copy-start | bytes 1540
  16.3 176.8 %copy-start.44 = (f32[128]{0:T(128)}, f32[128]{0:T(128)S(1)}, u32[]{:S(2)}) copy-start(f32[128]{0:T(128)S(1)} %get-tuple-element.134) | copy-start | bytes 1540
  193.4 8.3 collective-permute-start
  195.7 6.9 collective-permute-start.1
  202.8 211.3 %copy-start.7 = (f32[1536]{0:T(1024)S(1)}, f32[1536]{0:T(1024)}, u32[]{:S(2)}) copy-start(f32[1536]{0:T(1024)} %param.13) | copy-start | bytes 18436
  524.2 15.4 %copy-start.5 = (bf16[128,1536]{1,0:T(8,128)(2,1)S(1)}, bf16[128,1536]{1,0:T(8,128)(2,1)}, u32[]{:S(2)}) copy-start(bf16[128,1536]{1,0:T(8,128)(2,1)} %copy-done.4) | copy-start | bytes 1179652
  527.0 12.7 copy-start.9
  527.0 12.7 copy-start.10
  527.0 12.7 copy-start.11
  527.0 12.7 copy-start.13
  527.0 12.7 copy-start.15
  527.1 12.7 copy-start.17
  527.1 12.7 copy-start.19
  528.6 6.5 collective-permute-start.2
  532.6 6.9 collective-permute-start.3
  681.1 8.4 collective-permute-start.4
  685.2 6.9 collective-permute-start.5
  692.3 215.0 %copy-start.6 = (bf16[1,128,1536]{2,1,0:T(8,128)(2,1)S(1)}, bf16[1,128,1536]{2,1,0:T(8,128)(2,1)}, u32[]{:S(2)}) copy-start(bf16[1,128,1536]{2,1,0:T(8,128)(2,1)} %param.10) | copy-start | bytes 1179652
  (37 other events, 160.5 us)
Sparse Core Ops, SparseCore 0:
  11.3 174.8 all-gather.1
  1019.2 477.5 all-reduce.3

commit v2 on v1

--- a/solution.py
+++ b/solution.py
@@ -1,6 +1,8 @@
 import jax
 import jax.numpy as jnp
 from jax import lax
+from jax.experimental import pallas as pl
+from jax.experimental.pallas import tpu as pltpu
 from jax.sharding import PartitionSpec as P
 
 ASCENT = 2
@@ -23,6 +25,208 @@
     before = lax.ppermute(block[-half_span:], "tm", [(i, i + 1) for i in range(count - 1)])
     after = lax.ppermute(block[:half_span], "tm", [(i + 1, i) for i in range(count - 1)])
     return jnp.concatenate([before, block, after], axis=0).astype(jnp.float32)
+
+
+def place():
+    dp, tm = lax.axis_index("dp"), lax.axis_index("tm")
+    x, y_lo = dp // 2, lax.rem(dp, 2)
+    core, y_hi, z = lax.rem(tm, 2), lax.rem(tm // 2, 2), tm // 4
+    return x, y_hi * 2 + y_lo, z, core
+
+
+def device(x, y, z, core):
+    return (x * 2 + lax.rem(y, 2), (z * 2 + y // 2) * 2 + core)
+
+
+def groups():
+    x, y, z, core = place()
+    pair = (2, core, lambda i: device(x, y, z, i))
+    plane = (16, x * 4 + y, lambda i: device(i // 4, lax.rem(i, 4), z, core))
+    column = (16, z, lambda i: device(x, y, i, core))
+    quad = (4, (y // 2) * 2 + core, lambda i: device(x, (i // 2) * 2 + lax.rem(y, 2), z, lax.rem(i, 2)))
+    return pair, plane, column, quad
+
+
+def meet(*members):
+    barrier = pltpu.get_barrier_semaphore()
+    for count, mine, where in members:
+
+        def greet(d, carry):
+            pl.semaphore_signal(
+                barrier,
+                inc=1,
+                device_id=where(lax.rem(mine + d, count)),
+                device_id_type=pl.DeviceIdType.MESH,
+            )
+            return carry
+
+        lax.fori_loop(1, count, greet, 0)
+    pl.semaphore_wait(barrier, sum(count - 1 for count, _, _ in members))
+
+
+def exchange(group, source, landing, sems):
+    count, mine, where = group
+
+    def copy(d, out):
+        peer = lax.rem(mine + d, count)
+        slot = mine if out else peer
+        return pltpu.make_async_remote_copy(
+            src_ref=source(peer),
+            dst_ref=landing.at[slot],
+            send_sem=sems.at[0, d],
+            recv_sem=sems.at[1, slot],
+            device_id=where(peer),
+            device_id_type=pl.DeviceIdType.MESH,
+        )
+
+    def start(d, carry):
+        copy(d, True).start()
+        return carry
+
+    def finish(d, carry):
+        copy(d, False).wait_send()
+        copy(d, False).wait_recv()
+        return carry
+
+    lax.fori_loop(1, count, start, 0)
+    lax.fori_loop(1, count, finish, 0)
+
+
+def add_up(parts, count):
+    total = parts[0]
+    for i in range(1, count):
+        total = total + parts[i]
+    return total
+
+
+def join_moments(parts, count, sizes, stage):
+    half = parts.shape[1] // 2
+    total = parts[0, :half]
+    spread = parts[0, half:]
+    for i in range(1, count):
+        total = total + parts[i, :half]
+        spread = spread + parts[i, half:]
+    mean = total * sizes[stage, 2, 0]
+    for i in range(count):
+        apart = parts[i, :half] - sizes[stage, 0, i] * mean
+        spread = spread + apart * apart * sizes[stage, 1, i]
+    return jnp.concatenate([total, spread], axis=0)
+
+
+def sum_everywhere_kernel(moments, sizes, x_ref, out_ref, b0, b1, b2, b3, sems):
+    pair, plane, column, _ = groups()
+    meet(pair, plane, column)
+
+    def join(parts, count, stage):
+        return join_moments(parts, count, sizes, stage) if moments else add_up(parts, count)
+
+    core = pair[1]
+    b0[core] = x_ref[core]
+    exchange(pair, lambda peer: x_ref.at[peer], b0, sems.at[0])
+    b1[plane[1]] = join(b0, 2, 0)
+    exchange(plane, lambda peer: b1.at[plane[1]], b1, sems.at[1])
+    b2[column[1]] = join(b1, 16, 1)
+    exchange(column, lambda peer: b2.at[column[1]], b2, sems.at[2])
+    b3[core] = join(b2, 16, 2)
+    exchange(pair, lambda peer: b3.at[core], b3, sems.at[3])
+    out_ref[...] = b3[...]
+
+
+def sum_everywhere(first, second, sizes, moments, number):
+    packed = jnp.stack([first.reshape(2, 6, 128), second.reshape(2, 6, 128)], axis=1)
+    packed = jnp.pad(packed, ((0, 0), (0, 0), (0, 2), (0, 0))).reshape(2, 16, 128)
+    out = pl.pallas_call(
+        lambda *refs: sum_everywhere_kernel(moments, *refs),
+        out_shape=jax.ShapeDtypeStruct((2, 16, 128), jnp.float32),
+        in_specs=[
+            pl.BlockSpec(memory_space=pltpu.SMEM),
+            pl.BlockSpec(memory_space=pltpu.VMEM),
+        ],
+        out_specs=pl.BlockSpec(memory_space=pltpu.VMEM),
+        scratch_shapes=[
+            pltpu.VMEM((2, 16, 128), jnp.float32),
+            pltpu.VMEM((16, 16, 128), jnp.float32),
+            pltpu.VMEM((16, 16, 128), jnp.float32),
+            pltpu.VMEM((2, 16, 128), jnp.float32),
+            pltpu.SemaphoreType.DMA((4, 2, 16)),
+        ],
+        compiler_params=pltpu.CompilerParams(collective_id=number, has_side_effects=True),
+    )(sizes, packed)
+    out = out.reshape(2, 2, 8, 128)[:, :, :6]
+    return out[:, 0].reshape(-1), out[:, 1].reshape(-1)
+
+
+def group_sizes(ends, frame_rows):
+    x, y, z, core = place()
+    starts = frame_rows * jnp.arange(64, dtype=jnp.int32)
+    live = jnp.clip(ends[:, None] - starts[None, :], 0, frame_rows).astype(jnp.float32)
+    live = live.reshape(4, 2, 16, 2, 2).transpose(2, 0, 3, 1, 4).reshape(16, 16, 2)
+    here = lax.dynamic_index_in_dim(live, z, 0, keepdims=False)
+    pair = lax.dynamic_index_in_dim(here, x * 4 + y, 0, keepdims=False)
+    sizes = jnp.stack(
+        [jnp.pad(pair, (0, 14)), jnp.sum(here, axis=1), jnp.sum(live, axis=(1, 2))]
+    )
+    each = jnp.where(sizes > 0, 1.0 / jnp.maximum(sizes, 1.0), 0.0)
+    whole = jnp.sum(sizes, axis=1, keepdims=True)
+    whole = jnp.broadcast_to(1.0 / jnp.maximum(whole, 1.0), sizes.shape)
+    return jnp.stack([sizes, each, whole], axis=1)
+
+
+def square_sum_kernel(x_ref, out_ref, b0, b1, sems):
+    _, _, column, quad = groups()
+    meet(column, quad)
+    b0[column[1]] = x_ref[...]
+    exchange(column, lambda peer: b0.at[column[1]], b0, sems.at[0])
+    b1[quad[1]] = add_up(b0, 16)
+    exchange(quad, lambda peer: b1.at[quad[1]], b1, sems.at[1])
+    out_ref[...] = add_up(b1, 4)
+
+
+def square_sum(rows, number):
+    return pl.pallas_call(
+        square_sum_kernel,
+        out_shape=jax.ShapeDtypeStruct((8, 128), jnp.float32),
+        in_specs=[pl.BlockSpec(memory_space=pltpu.VMEM)],
+        out_specs=pl.BlockSpec(memory_space=pltpu.VMEM),
+        scratch_shapes=[
+            pltpu.VMEM((16, 8, 128), jnp.float32),
+            pltpu.VMEM((4, 8, 128), jnp.float32),
+            pltpu.SemaphoreType.DMA((2, 2, 16)),
+        ],
+        compiler_params=pltpu.CompilerParams(collective_id=number, has_side_effects=True),
+    )(rows)
+
+
+def scatter_taps_kernel(x_ref, out_ref, b0, b1, b2, s1, s2, sems):
+    pair, plane, column, _ = groups()
+    x, y, z, core = place()
+    meet(pair, plane, column)
+    exchange(pair, lambda peer: x_ref.at[peer], b0, sems.at[0])
+    s1[...] = x_ref[core] + b0[1 - core]
+    b1[z] = s1[z]
+    exchange(column, lambda peer: s1.at[peer], b1, sems.at[1])
+    s2[...] = add_up(b1, 16)
+    b2[plane[1]] = s2[y // 2]
+    exchange(plane, lambda peer: s2.at[lax.rem(peer, 4) // 2], b2, sems.at[2])
+    out_ref[...] = add_up(b2, 16)
+
+
+def scatter_taps(taps, number):
+    return pl.pallas_call(
+        scatter_taps_kernel,
+        out_shape=jax.ShapeDtypeStruct((8, 128), jnp.float32),
+        in_specs=[pl.BlockSpec(memory_space=pltpu.VMEM)],
+        out_specs=pl.BlockSpec(memory_space=pltpu.VMEM),
+        scratch_shapes=[
+            pltpu.VMEM((2, 16, 2, 8, 128), jnp.float32),
+            pltpu.VMEM((16, 2, 8, 128), jnp.float32),
+            pltpu.VMEM((16, 8, 128), jnp.float32),
+            pltpu.VMEM((16, 2, 8, 128), jnp.float32),
+            pltpu.VMEM((2, 8, 128), jnp.float32),
+            pltpu.SemaphoreType.DMA((3, 2, 16)),
+        ],
+        compiler_params=pltpu.CompilerParams(collective_id=number, has_side_effects=True),
+    )(taps)
 
 
 def conv(padded, kernel, out_length, flip):
@@ -56,7 +260,7 @@
     inputs = features[0].astype(jnp.float32)
     perturbation = noise_scale * start_noise[0].astype(jnp.float32) * live
     upstream = live * cotangent[0].astype(jnp.float32) / ASCENT
-    everywhere = ("dp", "tm")
+    sizes = group_sizes(ends, frame_rows)
     kernel_part = 0.0
     norm_part = 0.0
     for ascent_step in range(ASCENT):
@@ -73,16 +277,26 @@
         glu = (value_half * gate_half * live).astype(jnp.bfloat16)
         padded = with_halo(glu, half_span)
         conv_out = conv(padded, kernel, frame_rows, False)
-        batch_mean = lax.psum(jnp.sum(live * conv_out, axis=0), everywhere) / live_count
-        centred = conv_out - batch_mean
-        variance = lax.psum(jnp.sum(live * centred * centred, axis=0), everywhere) / live_count
+        local_sum = jnp.sum(live * conv_out, axis=0)
+        apart = conv_out - local_sum / jnp.maximum(jnp.sum(live), 1.0)
+        total, spread = sum_everywhere(
+            local_sum, jnp.sum(live * apart * apart, axis=0), sizes, True, 1 + 2 * ascent_step
+        )
+        centred = conv_out - total / live_count
+        variance = spread / live_count
         inv_std = lax.rsqrt(variance + batch_epsilon)
         scaled = centred * inv_std
         pre_act = bn_gain * scaled + bn_shift
         pre_sigmoid = jax.nn.sigmoid(pre_act)
         grad_pre = upstream * pre_sigmoid * (1.0 + pre_act * (1.0 - pre_sigmoid))
-        both = lax.psum(
-            jnp.stack([jnp.sum(grad_pre * scaled, axis=0), jnp.sum(grad_pre, axis=0)]), everywhere
+        both = jnp.stack(
+            sum_everywhere(
+                jnp.sum(grad_pre * scaled, axis=0),
+                jnp.sum(grad_pre, axis=0),
+                sizes,
+                False,
+                2 + 2 * ascent_step,
+            )
         )
         norm_part = norm_part + both
         grad_conv = (
@@ -107,18 +321,19 @@
                     - normed * jnp.mean(grad_normed * normed, axis=-1, keepdims=True)
                 )
             )
-            square_total = lax.psum(jnp.sum(direction * direction), "tm")
+            squares = jnp.sum((direction * direction).reshape(16, 8, 12, 128), axis=(0, 2))
+            square_total = jnp.sum(square_sum(squares, 5))
             perturbation = perturbation + direction * (
                 ascent_rate
                 * jnp.sqrt(utter_length * model_width)
                 / (jnp.sqrt(square_total) + ascent_epsilon)
             )
     width = model_width // lax.axis_size("tm")
-    by_shard = jnp.transpose(kernel_part.reshape(tap_count, -1, width), (1, 0, 2))
-    by_shard = jnp.pad(by_shard.reshape(by_shard.shape[0], -1), ((0, 0), (0, 24)))
-    kernel_total = lax.psum_scatter(by_shard.reshape(-1, 6, 128), "tm", scatter_dimension=0)
-    kernel_total = lax.psum(kernel_total, "dp").reshape(-1)[: tap_count * width]
-    kernel_total = kernel_total.reshape(tap_count, width)
+    by_shard = kernel_part.reshape(tap_count, 16, 2, 2, width).transpose(3, 1, 2, 0, 4)
+    by_shard = by_shard.reshape(64, tap_count * width)
+    by_shard = jnp.pad(by_shard, ((0, 0), (0, 1024 - tap_count * width)))
+    kernel_total = scatter_taps(by_shard.reshape(2, 16, 2, 8, 128), 6).reshape(-1)
+    kernel_total = kernel_total[: tap_count * width].reshape(tap_count, width)
     norm_total = lax.dynamic_slice_in_dim(norm_part, shard_index * width, width, 1)
     return (perturbation[None], kernel_total, norm_total)
 

time: 1540 us -> 478 us (0.31)
  blocking collectives: 767 us -> 0 us
  waiting for transfers between devices: 654 us -> 175 us
  Pallas kernels: 0 us -> 159 us
  local copies, waits for them, and re-layouts: 21.8 us -> 49.1 us
    psum x8 -> x0, blocking collectives: 767 us -> none  [the longest x2 217 us: on_device(): lax.psum(jnp.sum(live * conv_out, axis=0), everywhere) / live_count]
    unnamed x3 -> x1, waiting for transfers between devices: 476 us -> 0.68 us
    pallas_call x0 -> x6, Pallas kernels: none -> 159 us  [the longest x4 112 us: sum_everywhere(): pl.pallas_call(lambda *refs: sum_everywhere_kernel(moments, *refs), out_s...]
  transfers between devices with their start and end apart: 8 -> 7, of which waited for: 5 -> 3; matrix products, arithmetic and copies ran while one was open for 1% -> 6% of each run, Pallas kernels for 0% -> 0%
where the time goes in v2:
time: 478 us; the launch traced here: 475 us
  waiting for transfers between devices  175 us (37%)
  Pallas kernels  159 us (33%)
  local copies, waits for them, and re-layouts  49.1 us (10%)
  other arithmetic  41.8 us (9%)
  between operations  18.7 us (4%)
  starting transfers between devices  16.4 us (3%)
  matrix products  15.2 us (3%)
    all_gather x1, waiting for transfers between devices, on_device(): weight_full = lax.all_gather(in_weight, 'tm', axis=0, tiled=True)  168 us
    pallas_call x4, Pallas kernels, sum_everywhere(): pl.pallas_call(lambda *refs: sum_everywhere_kernel(moments, *refs), out_s...  112 us
    pallas_call x1, Pallas kernels, scatter_taps(): pl.pallas_call(scatter_taps_kernel, out_shape=jax.ShapeDtypeStruct((8, 12...  25.5 us
    pallas_call x1, Pallas kernels, square_sum(): pl.pallas_call(square_sum_kernel, out_shape=jax.ShapeDtypeStruct((8, 128)...  21.4 us
    unnamed x209, local copies, waits for them, and re-layouts  19 us
    another operation x64, local copies, waits for them, and re-layouts, tap_grad(): jnp.stack([jnp.sum(grad * padded[j:j + rows], axis=0) for j in range(taps)])  18.6 us
    dot_general x2, matrix products, on_device(): lax.dot_general(normed.astype(jnp.bfloat16), weight_full, (((1,), (1,)),...  13.7 us
    ppermute x3, starting transfers between devices, with_halo(): lax.ppermute(block[-half_span:], 'tm', [(i, i + 1) for i in range(count -...  10.1 us
  transfers between devices with their start and end apart: 7, of which 3 were waited for; matrix products, arithmetic and copies ran while one was open for 6% of the time, Pallas kernels for 0%

profile of v2, /device:TPU:1, one launch (start us, length us, event | category | flops | bytes accessed | tf_op | source)
XLA Modules:
  0.0 475.2 jit_solution(7118425962321734991)
XLA Ops:
  12.0 2.1 slice_reduce_fusion.29
  14.2 1.9 slice_reduce_fusion.30
  18.3 167.8 %all-gather.2.cloned.1.call-done = bf16[3072,1536]{1,0:T(8,128)(2,1)} async-done(((bf16[48,1536]{1,0:T(8,128)(2,1)}), bf16[3072,1536]{1,0:T(8,128)(2,1)}) %all-gather.2.cloned.1.call-update) | async-done | bytes 9437200 | tf_op jit(solution)/shard_map/all_gather | solution.py:259
  186.2 6.9 %fusion.122 = f32[128,3072]{1,0:T(8,128)S(1)} fusion(bf16[3072,1536]{1,0:T(8,128)(2,1)} %all-gather.2.cloned.1.call-done, bf16[1,128,1536]{2,1,0:T(8,128)(2,1)S(1)} %copy-done, bf16[1,128,1536]{2,1,0:T(8,128)(2,1)S(1)} %copy-done.2, f32[128]{0:T(128)S(1)} %get-tuple-element.142, f32[128]{0:T(128)S(1)} %broadcast_multiply_fusion.3, ...), kind=kOutput, calls=%fused_computation.247 | convolution fusion | flops 1209335808 | bytes 11798016 | tf_op jit(solution)/shard_map/dot_general | solution.py:269
  193.4 2.3 collective-permute-start
  195.7 2.0 collective-permute-start.1
  202.8 4.5 multiply_reduce_fusion.5
  210.2 30.3 %shard_map.103 = f32[2,16,128]{2,1,0:T(8,128)} custom-call(f32[3,3,16]{2,1,0:T(4,128)} %pad_maximum_fusion.4.refs_0_, f32[2,16,128]{2,1,0:T(8,128)} %pad_bitcast_fusion.4.refs_1_), custom_call_target="tpu_custom_call" | custom-call | tf_op jit(solution)/shard_map/pallas_call | solution.py:138
  241.2 2.4 multiply_reduce_fusion.4
  245.5 26.1 %shard_map.104 = f32[2,16,128]{2,1,0:T(8,128)} custom-call(f32[3,3,16]{2,1,0:T(4,128)} %pad_maximum_fusion.4.refs_0_, f32[2,16,128]{2,1,0:T(8,128)} %pad_bitcast_fusion.3.refs_1_), custom_call_target="tpu_custom_call" | custom-call | tf_op jit(solution)/shard_map/pallas_call | solution.py:138
  273.5 4.0 fusion.36
  294.4 4.6 collective-permute-start.2
  298.9 2.1 collective-permute-start.3
  317.9 3.3 fusion
  325.0 21.4 %shard_map.105 = f32[8,128]{1,0:T(8,128)} custom-call(f32[8,128]{1,0:T(8,128)} %get-tuple-element.115.x_ref), custom_call_target="tpu_custom_call" | custom-call | tf_op jit(solution)/shard_map/pallas_call | solution.py:186
  350.4 6.8 %fusion.124 = f32[128,3072]{1,0:T(8,128)S(1)} fusion(bf16[3072,1536]{1,0:T(8,128)(2,1)} %all-gather.2.cloned.1.call-done, f32[128,1536]{1,0:T(8,128)S(1)} %get-tuple-element.113, f32[128]{0:T(128)S(1)} %add_rsqrt_fusion, f32[128]{0:T(128)S(1)} %broadcast_multiply_fusion), kind=kOutput, calls=%fused_computation.248 | convolution fusion | flops 1208549376 | bytes 11797504 | tf_op jit(solution)/shard_map/dot_general | solution.py:269
  357.6 3.2 collective-permute-start.4
  360.9 2.1 collective-permute-start.5
  363.1 4.7 collective-permute-done.5
  368.0 3.1 multiply_reduce_fusion.1
  372.0 29.5 %shard_map.106 = f32[2,16,128]{2,1,0:T(8,128)} custom-call(f32[3,3,16]{2,1,0:T(4,128)} %pad_maximum_fusion.4.refs_0_, f32[2,16,128]{2,1,0:T(8,128)} %pad_bitcast_fusion.2.refs_1_), custom_call_target="tpu_custom_call" | custom-call | tf_op jit(solution)/shard_map/pallas_call | solution.py:138
  403.5 26.5 %shard_map.107 = f32[2,16,128]{2,1,0:T(8,128)} custom-call(f32[3,3,16]{2,1,0:T(4,128)} %pad_maximum_fusion.4.refs_0_, f32[2,16,128]{2,1,0:T(8,128)} %pad_bitcast_fusion.1.refs_1_), custom_call_target="tpu_custom_call" | custom-call | tf_op jit(solution)/shard_map/pallas_call | solution.py:138
  430.8 2.3 fusion.67
  440.7 25.5 %shard_map.108 = f32[8,128]{1,0:T(8,128)} custom-call(f32[2,16,2,8,128]{4,3,2,1,0:T(8,128)} %bitcast.132), custom_call_target="tpu_custom_call" | custom-call | tf_op jit(solution)/shard_map/pallas_call | solution.py:215
  (363 shorter events, 71.0 us)
Async XLA Ops:
  7.2 179.0 %all-gather.2.cloned.1.call-start = ((), (), s32[]{:S(2)}) async-start(), calls=%async_computation | async-start | bytes 9584640 | tf_op jit(solution)/shard_map/all_gather | solution.py:259
  11.2 181.9 %copy-start.39 = (f32[128]{0:T(128)}, f32[128]{0:T(128)S(1)}, u32[]{:S(2)}) copy-start(f32[128]{0:T(128)S(1)} %convert_element_type.94) | copy-start | bytes 1540
  14.1 188.6 %copy-start.10 = (f32[1536]{0:T(1024)}, f32[1536]{0:T(1024)S(1)}, u32[]{:S(2)}) copy-start(f32[1536]{0:T(1024)S(1)} %get-tuple-element.98) | copy-start | bytes 18436
  14.1 188.6 %copy-start.13 = (f32[1536]{0:T(1024)}, f32[1536]{0:T(1024)S(1)}, u32[]{:S(2)}) copy-start(f32[1536]{0:T(1024)S(1)} %get-tuple-element.99) | copy-start | bytes 18436
  14.1 188.6 %copy-start.16 = (f32[1536]{0:T(1024)}, f32[1536]{0:T(1024)S(1)}, u32[]{:S(2)}) copy-start(f32[1536]{0:T(1024)S(1)} %get-tuple-element.100) | copy-start | bytes 18436
  14.1 188.6 %copy-start.19 = (f32[1536]{0:T(1024)}, f32[1536]{0:T(1024)S(1)}, u32[]{:S(2)}) copy-start(f32[1536]{0:T(1024)S(1)} %get-tuple-element.101) | copy-start | bytes 18436
  16.1 177.1 %copy-start.61 = (f32[128]{0:T(128)}, f32[128]{0:T(128)S(1)}, u32[]{:S(2)}) copy-start(f32[128]{0:T(128)S(1)} %broadcast_select_fusion.1) | copy-start | bytes 1540
  17.5 175.6 %copy-start.65 = (f32[128]{0:T(128)}, f32[128]{0:T(128)S(1)}, u32[]{:S(2)}) copy-start(f32[128]{0:T(128)S(1)} %broadcast_multiply_fusion.3) | copy-start | bytes 1540
  18.3 174.8 %copy-start.63 = (f32[128]{0:T(128)}, f32[128]{0:T(128)S(1)}, u32[]{:S(2)}) copy-start(f32[128]{0:T(128)S(1)} %get-tuple-element.142) | copy-start | bytes 1540
  193.4 7.7 %collective-permute-start = (bf16[15,1536]{1,0:T(8,128)(2,1)S(1)}, bf16[15,1536]{1,0:T(8,128)(2,1)S(1)}, u32[]{:S(2)}, u32[]{:S(2)}) collective-permute-start(bf16[15,1536]{1,0:T(8,128)(2,1)S(1)} %get-tuple-element.129), channel_id=1, source_target_pairs={{0,1},{1,2},{2,3},{3,4},{4,5},{5,6},{6,7},{7,8},{8,9},{9,10},{10,1... | collective-permute-start | bytes 138248 | tf_op jit(solution)/shard_map/ppermute | solution.py:25
  195.7 6.9 %collective-permute-start.1 = (bf16[15,1536]{1,0:T(8,128)(2,1)S(1)}, bf16[15,1536]{1,0:T(8,128)(2,1)S(1)}, u32[]{:S(2)}, u32[]{:S(2)}) collective-permute-start(bf16[15,1536]{1,0:T(8,128)(2,1)S(1)} %get-tuple-element.130), channel_id=1, source_target_pairs={{1,0},{2,1},{3,2},{4,3},{5,4},{6,5},{7,6},{8,7},{9,8},{10,9},{11,1... | collective-permute-start | bytes 138248 | tf_op jit(solution)/shard_map/ppermute | solution.py:26
  202.8 38.4 %copy-start.9 = (f32[1536]{0:T(1024)S(1)}, f32[1536]{0:T(1024)}, u32[]{:S(2)}) copy-start(f32[1536]{0:T(1024)} %param.13) | copy-start | bytes 18436
  281.1 34.9 %copy-start.43 = (f32[1536]{0:T(1024)S(1)}, f32[1536]{0:T(1024)}, u32[]{:S(2)}) copy-start(f32[1536]{0:T(1024)} %get-tuple-element.40) | copy-start | bytes 18436
  281.2 35.5 %copy-start.5 = (bf16[128,1536]{1,0:T(8,128)(2,1)S(1)}, bf16[128,1536]{1,0:T(8,128)(2,1)}, u32[]{:S(2)}) copy-start(bf16[128,1536]{1,0:T(8,128)(2,1)} %copy-done.4) | copy-start | bytes 1179652
  294.4 22.3 %collective-permute-start.2 = (bf16[15,1536]{1,0:T(8,128)(2,1)}, bf16[15,1536]{1,0:T(8,128)(2,1)}, u32[]{:S(2)}, u32[]{:S(2)}) collective-permute-start(bf16[15,1536]{1,0:T(8,128)(2,1)} %get-tuple-element.127), channel_id=1, source_target_pairs={{0,1},{1,2},{2,3},{3,4},{4,5},{5,6},{6,7},{7,8},{8,9},{9,10},{10,1... | collective-permute-start | bytes 138248 | tf_op jit(solution)/shard_map/ppermute | solution.py:25
  298.9 17.7 %collective-permute-start.3 = (bf16[15,1536]{1,0:T(8,128)(2,1)}, bf16[15,1536]{1,0:T(8,128)(2,1)}, u32[]{:S(2)}, u32[]{:S(2)}) collective-permute-start(bf16[15,1536]{1,0:T(8,128)(2,1)} %get-tuple-element.128), channel_id=1, source_target_pairs={{1,0},{2,1},{3,2},{4,3},{5,4},{6,5},{7,6},{8,7},{9,8},{10,9},{11,1... | collective-permute-start | bytes 138248 | tf_op jit(solution)/shard_map/ppermute | solution.py:26
  303.4 14.4 %copy-start.11 = (f32[1536]{0:T(1024)S(1)}, f32[1536]{0:T(1024)}, u32[]{:S(2)}) copy-start(f32[1536]{0:T(1024)} %copy-done.10) | copy-start | bytes 18436
  303.4 14.4 %copy-start.14 = (f32[1536]{0:T(1024)S(1)}, f32[1536]{0:T(1024)}, u32[]{:S(2)}) copy-start(f32[1536]{0:T(1024)} %copy-done.13) | copy-start | bytes 18436
  303.4 14.4 %copy-start.17 = (f32[1536]{0:T(1024)S(1)}, f32[1536]{0:T(1024)}, u32[]{:S(2)}) copy-start(f32[1536]{0:T(1024)} %copy-done.16) | copy-start | bytes 18436
  303.4 14.4 %copy-start.20 = (f32[1536]{0:T(1024)S(1)}, f32[1536]{0:T(1024)}, u32[]{:S(2)}) copy-start(f32[1536]{0:T(1024)} %copy-done.19) | copy-start | bytes 18436
  357.6 5.5 %collective-permute-start.4 = (bf16[15,1536]{1,0:T(8,128)(2,1)S(1)}, bf16[15,1536]{1,0:T(8,128)(2,1)S(1)}, u32[]{:S(2)}, u32[]{:S(2)}) collective-permute-start(bf16[15,1536]{1,0:T(8,128)(2,1)S(1)} %get-tuple-element.125), channel_id=1, source_target_pairs={{0,1},{1,2},{2,3},{3,4},{4,5},{5,6},{6,7},{7,8},{8,9},{9,10},{10,1... | collective-permute-start | bytes 138248 | tf_op jit(solution)/shard_map/ppermute | solution.py:25
  360.9 6.9 %collective-permute-start.5 = (bf16[15,1536]{1,0:T(8,128)(2,1)S(1)}, bf16[15,1536]{1,0:T(8,128)(2,1)S(1)}, u32[]{:S(2)}, u32[]{:S(2)}) collective-permute-start(bf16[15,1536]{1,0:T(8,128)(2,1)S(1)} %get-tuple-element.126), channel_id=1, source_target_pairs={{1,0},{2,1},{3,2},{4,3},{5,4},{6,5},{7,6},{8,7},{9,8},{10,9},{11,1... | collective-permute-start | bytes 138248 | tf_op jit(solution)/shard_map/ppermute | solution.py:26
  368.0 34.3 %copy-start.6 = (bf16[1,128,1536]{2,1,0:T(8,128)(2,1)S(1)}, bf16[1,128,1536]{2,1,0:T(8,128)(2,1)}, u32[]{:S(2)}) copy-start(bf16[1,128,1536]{2,1,0:T(8,128)(2,1)} %param.10) | copy-start | bytes 1179652
  368.0 34.3 %copy-start.42 = (f32[1536]{0:T(1024)S(1)}, f32[1536]{0:T(1024)}, u32[]{:S(2)}) copy-start(f32[1536]{0:T(1024)} %param.14) | copy-start | bytes 18436
  (55 other events, 413.3 us)
Sparse Core Ops, SparseCore 0:
  11.3 174.8 all-gather.1

commit v3 on v2

--- a/solution.py
+++ b/solution.py
@@ -229,6 +229,185 @@
     )(taps)
 
 
+def gather_kernel(x_ref, out, column_sems, ring_sems, core_sems, own_sem):
+    x, y, z, core = place()
+    pair, _, column, _ = groups()
+    along_x = (4, x, lambda i: device(i, y, z, core))
+    along_y = (4, y, lambda i: device(x, i, z, core))
+    barrier = pltpu.get_barrier_semaphore()
+    near = [where(lax.rem(mine + d, 4)) for _, mine, where in (along_x, along_y) for d in (1, 3)]
+    for target in near + [pair[2](1 - core)]:
+        pl.semaphore_signal(
+            barrier, inc=1, device_id=target, device_id_type=pl.DeviceIdType.MESH
+        )
+
+    def greet(d, carry):
+        pl.semaphore_signal(
+            barrier,
+            inc=1,
+            device_id=column[2](lax.rem(z + d, 16)),
+            device_id_type=pl.DeviceIdType.MESH,
+        )
+        return carry
+
+    lax.fori_loop(1, 16, greet, 0)
+    pl.semaphore_wait(barrier, 20)
+
+    def lanes(i):
+        return pl.ds(pl.multiple_of(i * 384, 128), 384)
+
+    def rows(i):
+        return pl.ds(lax.rem(i, 2) * 3, 3)
+
+    def span(first, half):
+        return pl.ds(first, 8) if half is None else pl.ds(first + 4 * half, 4)
+
+    def first_x(i, half=None):
+        return out.at[span(0, half), y // 2, core, rows(y), :, lanes(i)]
+
+    def first_y(i, half=None):
+        return out.at[span(0, half), i // 2, core, rows(i)]
+
+    def second_y(i, half=None):
+        return out.at[span(8, half), i // 2, core, rows(i), :, lanes(x)]
+
+    def second_x(i, half=None):
+        return out.at[span(8, half), :, core, :, :, lanes(i)]
+
+    def remote(block, sems, number, target):
+        return pltpu.make_async_remote_copy(
+            src_ref=block,
+            dst_ref=block,
+            send_sem=sems.at[0, number],
+            recv_sem=sems.at[1, number],
+            device_id=target,
+            device_id_type=pl.DeviceIdType.MESH,
+        )
+
+    def piece(i):
+        return out.at[i, y // 2, core, rows(y), :, lanes(x)]
+
+    own = pltpu.make_async_copy(x_ref.at[rows(y), :, lanes(x)], piece(z), own_sem)
+    own.start()
+
+    def send(d, carry):
+        pltpu.make_async_remote_copy(
+            src_ref=x_ref.at[rows(y), :, lanes(x)],
+            dst_ref=piece(z),
+            send_sem=column_sems.at[0, d],
+            recv_sem=column_sems.at[1, z],
+            device_id=column[2](lax.rem(z + d, 16)),
+            device_id_type=pl.DeviceIdType.MESH,
+        ).start()
+        return carry
+
+    def take(d, carry):
+        peer = lax.rem(z + d, 16)
+        copy = pltpu.make_async_remote_copy(
+            src_ref=x_ref.at[rows(y), :, lanes(x)],
+            dst_ref=piece(peer),
+            send_sem=column_sems.at[0, d],
+            recv_sem=column_sems.at[1, peer],
+            device_id=column[2](peer),
+            device_id_type=pl.DeviceIdType.MESH,
+        )
+        copy.wait_send()
+        copy.wait_recv()
+        return carry
+
+    lax.fori_loop(1, 16, send, 0)
+    own.wait()
+    lax.fori_loop(1, 16, take, 0)
+
+    def ring(group, block, base, share=None):
+        _, mine, where = group
+        right, left, far = (lax.rem(mine + d, 4) for d in (1, 3, 2))
+        to_right, to_left = where(right), where(left)
+        sends = [
+            remote(block(mine), ring_sems, base, to_right),
+            remote(block(mine), ring_sems, base + 1, to_left),
+            remote(block(left, 0), ring_sems, base + 2, to_right),
+            remote(block(right, 1), ring_sems, base + 3, to_left),
+        ]
+        arrivals = [block(left), block(right), block(far, 0), block(far, 1)]
+        shared = []
+
+        def arrive(i):
+            remote(arrivals[i], ring_sems, base + i, to_left).wait_recv()
+            if share is not None:
+                give(arrivals[i], share + 1 + i)
+
+        def give(part, number):
+            copy = remote(part, core_sems, number, pair[2](1 - core))
+            copy.start()
+            shared.append(copy)
+
+        def begin():
+            sends[0].start()
+            sends[1].start()
+            if share is not None:
+                give(block(mine), share)
+
+        def middle():
+            arrive(0)
+            sends[2].start()
+            arrive(1)
+            sends[3].start()
+
+        def end():
+            arrive(2)
+            arrive(3)
+
+        def drain():
+            for copy in sends + shared:
+                copy.wait_send()
+
+        return begin, middle, end, drain
+
+    drains = []
+    for pass_rings in (
+        (ring(along_x, first_x, 0), ring(along_y, second_y, 4)),
+        (ring(along_y, first_y, 8, 0), ring(along_x, second_x, 12, 5)),
+    ):
+        for step in range(3):
+            for parts in pass_rings:
+                parts[step]()
+        drains += [parts[3] for parts in pass_rings]
+    for drain in drains:
+        drain()
+    other = 1 - core
+
+    def theirs_y(i, half=None):
+        return out.at[span(0, half), i // 2, other, rows(i)]
+
+    def theirs_x(i, half=None):
+        return out.at[span(8, half), :, other, :, :, lanes(i)]
+
+    for block, mine, base in ((theirs_y, y, 0), (theirs_x, x, 5)):
+        right, left, far = (lax.rem(mine + d, 4) for d in (1, 3, 2))
+        parts = [block(mine), block(left), block(right), block(far, 0), block(far, 1)]
+        for i, part in enumerate(parts):
+            remote(part, core_sems, base + i, pair[2](other)).wait_recv()
+
+
+def gather(weight, number):
+    shards = weight.shape[0] // 8
+    out = pl.pallas_call(
+        gather_kernel,
+        out_shape=jax.ShapeDtypeStruct((16, 2, 2, shards, 8, weight.shape[1]), weight.dtype),
+        in_specs=[pl.BlockSpec(memory_space=pltpu.VMEM)],
+        out_specs=pl.BlockSpec(memory_space=pl.ANY),
+        scratch_shapes=[
+            pltpu.SemaphoreType.DMA((2, 16)),
+            pltpu.SemaphoreType.DMA((2, 16)),
+            pltpu.SemaphoreType.DMA((2, 10)),
+            pltpu.SemaphoreType.DMA,
+        ],
+        compiler_params=pltpu.CompilerParams(collective_id=number, has_side_effects=True),
+    )(weight.reshape(shards, 8, -1))
+    return out.reshape(-1, weight.shape[1])
+
+
 def conv(padded, kernel, out_length, flip):
     taps = kernel.shape[0]
     result = None
@@ -256,7 +435,7 @@
     utter_length = utter_end.astype(jnp.float32)
     frame_ids = shard_index * frame_rows + jnp.arange(frame_rows, dtype=jnp.int32)
     live = (frame_ids < utter_end).astype(jnp.float32)[:, None]
-    weight_full = lax.all_gather(in_weight, "tm", axis=0, tiled=True)
+    weight_full = gather(in_weight, 7)
     inputs = features[0].astype(jnp.float32)
     perturbation = noise_scale * start_noise[0].astype(jnp.float32) * live
     upstream = live * cotangent[0].astype(jnp.float32) / ASCENT

time: 478 us -> 363 us (0.76)
  waiting for transfers between devices: 175 us -> 3.44 us
  Pallas kernels: 159 us -> 230 us
  between operations: 18.7 us -> 5.27 us
    all_gather x1 -> x0, waiting for transfers between devices: 168 us -> none  [on_device(): weight_full = lax.all_gather(in_weight, 'tm', axis=0, tiled=True)]
    pallas_call x0 -> x1, Pallas kernels: none -> 67.8 us  [gather(): pl.pallas_call(gather_kernel, out_shape=jax.ShapeDtypeStruct((16, 2, 2, s...]
    unnamed x209 -> x215, local copies, waits for them, and re-layouts: 19 us -> 19 us
  transfers between devices with their start and end apart: 7 -> 6, of which waited for: 3 -> 1; matrix products, arithmetic and copies ran while one was open for 6% -> 6% of each run, Pallas kernels for 0% -> 0%
where the time goes in v3:
time: 363 us; the launch traced here: 361 us
  Pallas kernels  230 us (63%)
  local copies, waits for them, and re-layouts  46.8 us (13%)
  other arithmetic  42.9 us (12%)
  starting transfers between devices  17.4 us (5%)
  matrix products  15.2 us (4%)
  between operations  5.27 us (1%)
    pallas_call x4, Pallas kernels, sum_everywhere(): pl.pallas_call(lambda *refs: sum_everywhere_kernel(moments, *refs), out_s...  114 us
    pallas_call x1, Pallas kernels, gather(): pl.pallas_call(gather_kernel, out_shape=jax.ShapeDtypeStruct((16, 2, 2, s...  67.8 us
    pallas_call x1, Pallas kernels, scatter_taps(): pl.pallas_call(scatter_taps_kernel, out_shape=jax.ShapeDtypeStruct((8, 12...  26.1 us
    pallas_call x1, Pallas kernels, square_sum(): pl.pallas_call(square_sum_kernel, out_shape=jax.ShapeDtypeStruct((8, 128)...  22 us
    unnamed x215, local copies, waits for them, and re-layouts  19 us
    another operation x64, local copies, waits for them, and re-layouts, tap_grad(): jnp.stack([jnp.sum(grad * padded[j:j + rows], axis=0) for j in range(taps)])  18.6 us
    dot_general x2, matrix products, on_device(): lax.dot_general(normed.astype(jnp.bfloat16), weight_full, (((1,), (1,)),...  13.7 us
    ppermute x3, starting transfers between devices, with_halo(): lax.ppermute(block[-half_span:], 'tm', [(i, i + 1) for i in range(count -...  11 us
  transfers between devices with their start and end apart: 6, of which 1 were waited for; matrix products, arithmetic and copies ran while one was open for 6% of the time, Pallas kernels for 0%

profile of v3, /device:TPU:1, one launch (start us, length us, event | category | flops | bytes accessed | tf_op | source)
XLA Modules:
  0.0 360.8 jit_solution(17831916906580358165)
XLA Ops:
  6.5 67.8 %shard_map.103 = bf16[16,2,2,6,8,1536]{5,4,3,2,1,0:T(8,128)(2,1)} custom-call(bf16[6,8,1536]{2,1,0:T(8,128)(2,1)} %bitcast.157), custom_call_target="tpu_custom_call" | custom-call | tf_op jit(solution)/shard_map/pallas_call | solution.py:395
  74.4 6.9 %fusion.130 = f32[128,3072]{1,0:T(8,128)S(1)} fusion(bf16[3072,1536]{1,0:T(8,128)(2,1)} %bitcast.150, bf16[1,128,1536]{2,1,0:T(8,128)(2,1)S(1)} %copy-done, bf16[1,128,1536]{2,1,0:T(8,128)(2,1)S(1)} %copy-done.2, f32[128]{0:T(128)S(1)} %get-tuple-element.142, f32[128]{0:T(128)S(1)} %broadcast_multiply_fusion.3, f32[128]{0:T(128)S(1)} %broadcast_select_fusion.1), kind=kOutput, calls=%fused_computation.255 | convolution fusion | flops 1209335808 | bytes 11798016 | tf_op jit(solution)/shard_map/dot_general | solution.py:448
  81.6 2.7 collective-permute-start
  84.3 2.1 collective-permute-start.1
  92.0 4.5 %multiply_reduce_fusion.5 = (f32[1536]{0:T(1024)}, f32[128,1536]{1,0:T(8,128)S(1)}) fusion(f32[128]{0:T(128)} %copy-done.40, f32[158,1536]{1,0:T(8,128)S(1)} %maximum_convert_fusion, f32[1536]{0:T(1024)} %get-tuple-element.106, f32[1536]{0:T(1024)} %get-tuple-element.107, f32[1536]{0:T(1024)S(1)} %get-tuple-element.78, f32[1536]{0:T(1024)S(1)} %get-tuple-element.79, ...), kind=kLoop, calls=%fused_computation.242 | loop fusion | flops 12384768 | bytes 25362944 | tf_op jit(solution)/shard_map/reduce_sum | solution.py:459
  99.4 29.1 %shard_map.104 = f32[2,16,128]{2,1,0:T(8,128)} custom-call(f32[3,3,16]{2,1,0:T(4,128)} %pad_maximum_fusion.4.refs_0_, f32[2,16,128]{2,1,0:T(8,128)} %pad_bitcast_fusion.4.refs_1_), custom_call_target="tpu_custom_call" | custom-call | tf_op jit(solution)/shard_map/pallas_call | solution.py:138
  129.3 2.4 multiply_reduce_fusion.4
  133.6 28.2 %shard_map.105 = f32[2,16,128]{2,1,0:T(8,128)} custom-call(f32[3,3,16]{2,1,0:T(4,128)} %pad_maximum_fusion.4.refs_0_, f32[2,16,128]{2,1,0:T(8,128)} %pad_bitcast_fusion.3.refs_1_), custom_call_target="tpu_custom_call" | custom-call | tf_op jit(solution)/shard_map/pallas_call | solution.py:138
  163.7 4.0 %fusion.43 = (f32[1536]{0:T(1024)}, f32[1536]{0:T(1024)}, f32[1536]{0:T(1024)}, f32[1536]{0:T(1024)}, f32[1536]{0:T(1024)}, /*index=5*/f32[1536]{0:T(1024)}, f32...) fusion(f32[158,1536]{1,0:T(8,128)S(1)} %maximum_convert_fusion,, ...), kind=kLoop, calls=%fused_computation.114 | loop fusion | flops 9212928 | bytes 16263684 | tf_op jit(solution)/shard_map/reduce_sum | solution.py:423
  184.6 3.3 collective-permute-start.2
  187.9 2.1 collective-permute-start.3
  206.9 3.3 fusion.2
  211.3 1.5 fusion.152
  214.0 22.0 %shard_map.106 = f32[8,128]{1,0:T(8,128)} custom-call(f32[8,128]{1,0:T(8,128)} %get-tuple-element.115.x_ref), custom_call_target="tpu_custom_call" | custom-call | tf_op jit(solution)/shard_map/pallas_call | solution.py:186
  238.0 1.8 fusion.154
  240.1 6.8 %fusion.128 = f32[128,3072]{1,0:T(8,128)S(1)} fusion(bf16[3072,1536]{1,0:T(8,128)(2,1)} %bitcast.151, f32[128,1536]{1,0:T(8,128)S(1)} %get-tuple-element.113, f32[128]{0:T(128)S(1)} %add_rsqrt_fusion, f32[128]{0:T(128)S(1)} %broadcast_multiply_fusion), kind=kOutput, calls=%fused_computation.253 | convolution fusion | flops 1208549376 | bytes 11797504 | tf_op jit(solution)/shard_map/dot_general | solution.py:448
  247.3 5.0 %collective-permute-start.4 = (bf16[15,1536]{1,0:T(8,128)(2,1)S(1)}, bf16[15,1536]{1,0:T(8,128)(2,1)S(1)}, u32[]{:S(2)}, u32[]{:S(2)}) collective-permute-start(bf16[15,1536]{1,0:T(8,128)(2,1)S(1)} %get-tuple-element.125), channel_id=1, source_target_pairs={{0,1},{1,2},{2,3},{3,4},{4,5},{5,6},{6,7},{7,8},{8,9},{9,10},{10,1... | collective-permute-start | bytes 138248 | tf_op jit(solution)/shard_map/ppermute | solution.py:25
  252.3 2.2 collective-permute-start.5
  255.7 3.4 collective-permute-done.5
  259.4 3.1 multiply_reduce_fusion.1
  263.4 29.4 %shard_map.107 = f32[2,16,128]{2,1,0:T(8,128)} custom-call(f32[3,3,16]{2,1,0:T(4,128)} %pad_maximum_fusion.4.refs_0_, f32[2,16,128]{2,1,0:T(8,128)} %pad_bitcast_fusion.2.refs_1_), custom_call_target="tpu_custom_call" | custom-call | tf_op jit(solution)/shard_map/pallas_call | solution.py:138
  294.7 27.1 %shard_map.108 = f32[2,16,128]{2,1,0:T(8,128)} custom-call(f32[3,3,16]{2,1,0:T(4,128)} %pad_maximum_fusion.4.refs_0_, f32[2,16,128]{2,1,0:T(8,128)} %pad_bitcast_fusion.1.refs_1_), custom_call_target="tpu_custom_call" | custom-call | tf_op jit(solution)/shard_map/pallas_call | solution.py:138
  322.6 2.3 fusion.74
  332.5 26.1 %shard_map.109 = f32[8,128]{1,0:T(8,128)} custom-call(f32[2,16,2,8,128]{4,3,2,1,0:T(8,128)} %bitcast.155), custom_call_target="tpu_custom_call" | custom-call | tf_op jit(solution)/shard_map/pallas_call | solution.py:215
  (367 shorter events, 68.2 us)
Async XLA Ops:
  3.1 78.2 %copy-start.40 = (f32[128]{0:T(128)}, f32[128]{0:T(128)S(1)}, u32[]{:S(2)}) copy-start(f32[128]{0:T(128)S(1)} %convert_element_type.103) | copy-start | bytes 1540
  3.1 71.2 %copy-start.64 = (f32[128]{0:T(128)}, f32[128]{0:T(128)S(1)}, u32[]{:S(2)}) copy-start(f32[128]{0:T(128)S(1)} %broadcast_select_fusion.1) | copy-start | bytes 1540
  4.5 69.8 %copy-start.68 = (f32[128]{0:T(128)}, f32[128]{0:T(128)S(1)}, u32[]{:S(2)}) copy-start(f32[128]{0:T(128)S(1)} %broadcast_multiply_fusion.3) | copy-start | bytes 1540
  6.5 67.9 %copy-start.66 = (f32[128]{0:T(128)}, f32[128]{0:T(128)S(1)}, u32[]{:S(2)}) copy-start(f32[128]{0:T(128)S(1)} %get-tuple-element.142) | copy-start | bytes 1540
  6.5 67.9 %copy-start = (bf16[1,128,1536]{2,1,0:T(8,128)(2,1)S(1)}, bf16[1,128,1536]{2,1,0:T(8,128)(2,1)}, u32[]{:S(2)}) copy-start(bf16[1,128,1536]{2,1,0:T(8,128)(2,1)} %param.9) | copy-start | bytes 1179652
  6.5 67.9 %copy-start.2 = (bf16[1,128,1536]{2,1,0:T(8,128)(2,1)S(1)}, bf16[1,128,1536]{2,1,0:T(8,128)(2,1)}, u32[]{:S(2)}) copy-start(bf16[1,128,1536]{2,1,0:T(8,128)(2,1)} %param.8) | copy-start | bytes 1179652
  81.6 10.2 %collective-permute-start = (bf16[15,1536]{1,0:T(8,128)(2,1)S(1)}, bf16[15,1536]{1,0:T(8,128)(2,1)S(1)}, u32[]{:S(2)}, u32[]{:S(2)}) collective-permute-start(bf16[15,1536]{1,0:T(8,128)(2,1)S(1)} %get-tuple-element.129), channel_id=1, source_target_pairs={{0,1},{1,2},{2,3},{3,4},{4,5},{5,6},{6,7},{7,8},{8,9},{9,10},{10,1... | collective-permute-start | bytes 138248 | tf_op jit(solution)/shard_map/ppermute | solution.py:25
  84.3 7.5 %collective-permute-start.1 = (bf16[15,1536]{1,0:T(8,128)(2,1)S(1)}, bf16[15,1536]{1,0:T(8,128)(2,1)S(1)}, u32[]{:S(2)}, u32[]{:S(2)}) collective-permute-start(bf16[15,1536]{1,0:T(8,128)(2,1)S(1)} %get-tuple-element.130), channel_id=1, source_target_pairs={{1,0},{2,1},{3,2},{4,3},{5,4},{6,5},{7,6},{8,7},{9,8},{10,9},{11,1... | collective-permute-start | bytes 138248 | tf_op jit(solution)/shard_map/ppermute | solution.py:26
  92.0 37.3 %copy-start.10 = (f32[1536]{0:T(1024)S(1)}, f32[1536]{0:T(1024)}, u32[]{:S(2)}) copy-start(f32[1536]{0:T(1024)} %param.13) | copy-start | bytes 18436
  171.3 33.6 %copy-start.44 = (f32[1536]{0:T(1024)S(1)}, f32[1536]{0:T(1024)}, u32[]{:S(2)}) copy-start(f32[1536]{0:T(1024)} %get-tuple-element.40) | copy-start | bytes 18436
  171.4 34.2 %copy-start.5 = (bf16[128,1536]{1,0:T(8,128)(2,1)S(1)}, bf16[128,1536]{1,0:T(8,128)(2,1)}, u32[]{:S(2)}) copy-start(bf16[128,1536]{1,0:T(8,128)(2,1)} %copy-done.4) | copy-start | bytes 1179652
  184.6 21.1 %collective-permute-start.2 = (bf16[15,1536]{1,0:T(8,128)(2,1)}, bf16[15,1536]{1,0:T(8,128)(2,1)}, u32[]{:S(2)}, u32[]{:S(2)}) collective-permute-start(bf16[15,1536]{1,0:T(8,128)(2,1)} %get-tuple-element.127), channel_id=1, source_target_pairs={{0,1},{1,2},{2,3},{3,4},{4,5},{5,6},{6,7},{7,8},{8,9},{9,10},{10,1... | collective-permute-start | bytes 138248 | tf_op jit(solution)/shard_map/ppermute | solution.py:25
  187.9 17.7 %collective-permute-start.3 = (bf16[15,1536]{1,0:T(8,128)(2,1)}, bf16[15,1536]{1,0:T(8,128)(2,1)}, u32[]{:S(2)}, u32[]{:S(2)}) collective-permute-start(bf16[15,1536]{1,0:T(8,128)(2,1)} %get-tuple-element.128), channel_id=1, source_target_pairs={{1,0},{2,1},{3,2},{4,3},{5,4},{6,5},{7,6},{8,7},{9,8},{10,9},{11,1... | collective-permute-start | bytes 138248 | tf_op jit(solution)/shard_map/ppermute | solution.py:26
  192.4 14.4 %copy-start.12 = (f32[1536]{0:T(1024)S(1)}, f32[1536]{0:T(1024)}, u32[]{:S(2)}) copy-start(f32[1536]{0:T(1024)} %copy-done.11) | copy-start | bytes 18436
  192.4 14.4 %copy-start.15 = (f32[1536]{0:T(1024)S(1)}, f32[1536]{0:T(1024)}, u32[]{:S(2)}) copy-start(f32[1536]{0:T(1024)} %copy-done.14) | copy-start | bytes 18436
  192.4 14.4 %copy-start.18 = (f32[1536]{0:T(1024)S(1)}, f32[1536]{0:T(1024)}, u32[]{:S(2)}) copy-start(f32[1536]{0:T(1024)} %copy-done.17) | copy-start | bytes 18436
  192.4 14.4 %copy-start.21 = (f32[1536]{0:T(1024)S(1)}, f32[1536]{0:T(1024)}, u32[]{:S(2)}) copy-start(f32[1536]{0:T(1024)} %copy-done.20) | copy-start | bytes 18436
  192.4 14.4 %copy-start.23 = (f32[1536]{0:T(1024)S(1)}, f32[1536]{0:T(1024)}, u32[]{:S(2)}) copy-start(f32[1536]{0:T(1024)} %get-tuple-element.102) | copy-start | bytes 18436
  247.3 8.5 %collective-permute-start.4 = (bf16[15,1536]{1,0:T(8,128)(2,1)S(1)}, bf16[15,1536]{1,0:T(8,128)(2,1)S(1)}, u32[]{:S(2)}, u32[]{:S(2)}) collective-permute-start(bf16[15,1536]{1,0:T(8,128)(2,1)S(1)} %get-tuple-element.125), channel_id=1, source_target_pairs={{0,1},{1,2},{2,3},{3,4},{4,5},{5,6},{6,7},{7,8},{8,9},{9,10},{10,1... | collective-permute-start | bytes 138248 | tf_op jit(solution)/shard_map/ppermute | solution.py:25
  252.3 6.9 %collective-permute-start.5 = (bf16[15,1536]{1,0:T(8,128)(2,1)S(1)}, bf16[15,1536]{1,0:T(8,128)(2,1)S(1)}, u32[]{:S(2)}, u32[]{:S(2)}) collective-permute-start(bf16[15,1536]{1,0:T(8,128)(2,1)S(1)} %get-tuple-element.126), channel_id=1, source_target_pairs={{1,0},{2,1},{3,2},{4,3},{5,4},{6,5},{7,6},{8,7},{9,8},{10,9},{11,1... | collective-permute-start | bytes 138248 | tf_op jit(solution)/shard_map/ppermute | solution.py:26
  259.4 34.1 %copy-start.6 = (bf16[1,128,1536]{2,1,0:T(8,128)(2,1)S(1)}, bf16[1,128,1536]{2,1,0:T(8,128)(2,1)}, u32[]{:S(2)}) copy-start(bf16[1,128,1536]{2,1,0:T(8,128)(2,1)} %param.10) | copy-start | bytes 1179652
  259.4 34.1 %copy-start.43 = (f32[1536]{0:T(1024)S(1)}, f32[1536]{0:T(1024)}, u32[]{:S(2)}) copy-start(f32[1536]{0:T(1024)} %param.14) | copy-start | bytes 18436
  331.2 28.9 %copy-start.62 = (f32[1,1536]{1,0:T(1,128)S(1)}, f32[1,1536]{1,0:T(1,128)}, u32[]{:S(2)}) copy-start(f32[1,1536]{1,0:T(1,128)} %stack_reshape_squeeze.13) | copy-start | bytes 18436
  331.2 28.9 %copy-start.63 = (f32[1,1536]{1,0:T(1,128)S(1)}, f32[1,1536]{1,0:T(1,128)}, u32[]{:S(2)}) copy-start(f32[1,1536]{1,0:T(1,128)} %stack_reshape_squeeze.12) | copy-start | bytes 18436
  (57 other events, 446.5 us)

commit v4 on v3

--- a/solution.py
+++ b/solution.py
@@ -113,59 +113,127 @@
     return jnp.concatenate([total, spread], axis=0)
 
 
-def sum_everywhere_kernel(moments, sizes, x_ref, out_ref, b0, b1, b2, b3, sems):
-    pair, plane, column, _ = groups()
-    meet(pair, plane, column)
-
-    def join(parts, count, stage):
-        return join_moments(parts, count, sizes, stage) if moments else add_up(parts, count)
-
-    core = pair[1]
-    b0[core] = x_ref[core]
-    exchange(pair, lambda peer: x_ref.at[peer], b0, sems.at[0])
-    b1[plane[1]] = join(b0, 2, 0)
-    exchange(plane, lambda peer: b1.at[plane[1]], b1, sems.at[1])
-    b2[column[1]] = join(b1, 16, 1)
-    exchange(column, lambda peer: b2.at[column[1]], b2, sems.at[2])
-    b3[core] = join(b2, 16, 2)
-    exchange(pair, lambda peer: b3.at[core], b3, sems.at[3])
-    out_ref[...] = b3[...]
-
-
-def sum_everywhere(first, second, sizes, moments, number):
-    packed = jnp.stack([first.reshape(2, 6, 128), second.reshape(2, 6, 128)], axis=1)
-    packed = jnp.pad(packed, ((0, 0), (0, 0), (0, 2), (0, 0))).reshape(2, 16, 128)
-    out = pl.pallas_call(
-        lambda *refs: sum_everywhere_kernel(moments, *refs),
-        out_shape=jax.ShapeDtypeStruct((2, 16, 128), jnp.float32),
-        in_specs=[
-            pl.BlockSpec(memory_space=pltpu.SMEM),
-            pl.BlockSpec(memory_space=pltpu.VMEM),
-        ],
-        out_specs=pl.BlockSpec(memory_space=pltpu.VMEM),
+def flat_plane():
+    x, y, z, core = place()
+    return (
+        32,
+        (x * 4 + y) * 2 + core,
+        lambda i: device(i // 8, lax.rem(i // 2, 4), z, lax.rem(i, 2)),
+    )
+
+
+def sum_everywhere(src, b1, b2, b3, sems, join):
+    plane, column = flat_plane(), groups()[2]
+    me, z = plane[1], column[1]
+    b1[me] = src[me]
+    exchange(plane, lambda peer: src.at[peer], b1, sems.at[0])
+    b2[z] = join(b1, 32, 0)
+    exchange(column, lambda peer: b2.at[z], b2, sems.at[1])
+    b3[me] = join(b2, 16, 1)
+    exchange(plane, lambda peer: b3.at[me], b3, sems.at[2])
+
+
+def batch_norm_kernel(
+    sizes, counts, conv_ref, up_ref, live_ref, padded_ref, gain_ref, shift_ref,
+    grad_ref, both_ref, taps_ref,
+    scaled_ref, pre_ref, inv_ref, s1, a1, a2, a3, s2, c1, c2, c3, sems1, sems2,
+):
+    meet(flat_plane(), groups()[2])
+    tiles = conv_ref.shape[1] // 128
+    rows = conv_ref.shape[0]
+    total_live = counts[1]
+
+    def at(i):
+        return pl.ds(pl.multiple_of(i * 128, 128), 128)
+
+    def each(body):
+        def step(i, carry):
+            body(i)
+            return carry
+
+        lax.fori_loop(0, tiles, step, 0)
+
+    s1[...] = jnp.zeros(s1.shape, jnp.float32)
+    s2[...] = jnp.zeros(s2.shape, jnp.float32)
+
+    def moments(i):
+        part, live = conv_ref[:, at(i)], live_ref[...]
+        local = jnp.sum(part * live, axis=0, keepdims=True)
+        apart = part - local * counts[0]
+        s1[i, 0:1] = local
+        s1[i, 1:2] = jnp.sum(live * apart * apart, axis=0, keepdims=True)
+
+    each(moments)
+    sum_everywhere(s1, a1, a2, a3, sems1, lambda p, n, k: join_moments(p, n, sizes, k))
+
+    def activate(i):
+        found = a3[i]
+        inv_std = lax.rsqrt(found[1:2] / total_live + batch_epsilon)
+        scaled = (conv_ref[:, at(i)] - found[0:1] / total_live) * inv_std
+        pre_act = gain_ref[:, at(i)] * scaled + shift_ref[:, at(i)]
+        pre_sigmoid = jax.nn.sigmoid(pre_act)
+        grad_pre = up_ref[:, at(i)] * pre_sigmoid * (1.0 + pre_act * (1.0 - pre_sigmoid))
+        scaled_ref[:, at(i)] = scaled
+        pre_ref[:, at(i)] = grad_pre
+        inv_ref[:, at(i)] = inv_std
+        s2[i, 0:1] = jnp.sum(grad_pre * scaled, axis=0, keepdims=True)
+        s2[i, 1:2] = jnp.sum(grad_pre, axis=0, keepdims=True)
+
+    each(activate)
+    sum_everywhere(s2, c1, c2, c3, sems2, lambda p, n, k: add_up(p, n))
+
+    def backward(i):
+        found = c3[i]
+        both_ref[:, at(i)] = found
+        scaled, grad_pre = scaled_ref[:, at(i)], pre_ref[:, at(i)]
+        grad = (
+            live_ref[...]
+            * (inv_ref[:, at(i)] * gain_ref[:, at(i)])
+            * (grad_pre - (found[1:2] + scaled * found[0:1]) / total_live)
+        ).astype(jnp.bfloat16)
+        grad_ref[:, at(i)] = grad
+        grad = grad.astype(jnp.float32)
+        for j in range(31):
+            window = padded_ref[pl.ds(j, rows), at(i)]
+            taps_ref[pl.ds(j, 1), at(i)] = jnp.sum(grad * window, axis=0, keepdims=True)
+        taps_ref[pl.ds(31, 1), at(i)] = jnp.zeros((1, 128), jnp.float32)
+
+    each(backward)
+
+
+def batch_norm(sizes, counts, conv_out, upstream, live, padded, gain, shift, number):
+    rows, width = conv_out.shape
+    smem, vmem = pl.BlockSpec(memory_space=pltpu.SMEM), pl.BlockSpec(memory_space=pltpu.VMEM)
+    slots = [pltpu.VMEM((n, 2, 128), jnp.float32) for n in (32, 32, 16, 32)]
+    return pl.pallas_call(
+        batch_norm_kernel,
+        out_shape=(
+            jax.ShapeDtypeStruct((rows, width), jnp.bfloat16),
+            jax.ShapeDtypeStruct((2, width), jnp.float32),
+            jax.ShapeDtypeStruct((32, width), jnp.float32),
+        ),
+        in_specs=[smem, smem] + [vmem] * 6,
+        out_specs=(vmem, vmem, vmem),
         scratch_shapes=[
-            pltpu.VMEM((2, 16, 128), jnp.float32),
-            pltpu.VMEM((16, 16, 128), jnp.float32),
-            pltpu.VMEM((16, 16, 128), jnp.float32),
-            pltpu.VMEM((2, 16, 128), jnp.float32),
-            pltpu.SemaphoreType.DMA((4, 2, 16)),
-        ],
+            pltpu.VMEM((rows, width), jnp.float32),
+            pltpu.VMEM((rows, width), jnp.float32),
+            pltpu.VMEM((1, width), jnp.float32),
+        ]
+        + slots
+        + slots
+        + [pltpu.SemaphoreType.DMA((3, 2, 32)), pltpu.SemaphoreType.DMA((3, 2, 32))],
         compiler_params=pltpu.CompilerParams(collective_id=number, has_side_effects=True),
-    )(sizes, packed)
-    out = out.reshape(2, 2, 8, 128)[:, :, :6]
-    return out[:, 0].reshape(-1), out[:, 1].reshape(-1)
+    )(sizes, counts, conv_out, upstream, jnp.broadcast_to(live, (rows, 128)), padded,
+      gain[None], shift[None])
 
 
 def group_sizes(ends, frame_rows):
-    x, y, z, core = place()
+    _, _, z, _ = place()
     starts = frame_rows * jnp.arange(64, dtype=jnp.int32)
     live = jnp.clip(ends[:, None] - starts[None, :], 0, frame_rows).astype(jnp.float32)
-    live = live.reshape(4, 2, 16, 2, 2).transpose(2, 0, 3, 1, 4).reshape(16, 16, 2)
+    live = live.reshape(4, 2, 16, 2, 2).transpose(2, 0, 3, 1, 4).reshape(16, 32)
     here = lax.dynamic_index_in_dim(live, z, 0, keepdims=False)
-    pair = lax.dynamic_index_in_dim(here, x * 4 + y, 0, keepdims=False)
-    sizes = jnp.stack(
-        [jnp.pad(pair, (0, 14)), jnp.sum(here, axis=1), jnp.sum(live, axis=(1, 2))]
-    )
+    sizes = jnp.stack([here, jnp.pad(jnp.sum(live, axis=1), (0, 16))])
     each = jnp.where(sizes > 0, 1.0 / jnp.maximum(sizes, 1.0), 0.0)
     whole = jnp.sum(sizes, axis=1, keepdims=True)
     whole = jnp.broadcast_to(1.0 / jnp.maximum(whole, 1.0), sizes.shape)
@@ -416,11 +484,6 @@
         term = kernel[offset] * padded[start : start + out_length]
         result = term if result is None else result + term
     return result
-
-
-def tap_grad(grad, padded, taps):
-    rows = grad.shape[0]
-    return jnp.stack([jnp.sum(grad * padded[j : j + rows], axis=0) for j in range(taps)])
 
 
 def on_device(features, start_noise, cotangent, in_weight, kernel, bn_gain, bn_shift, ends):
@@ -440,6 +503,7 @@
     perturbation = noise_scale * start_noise[0].astype(jnp.float32) * live
     upstream = live * cotangent[0].astype(jnp.float32) / ASCENT
     sizes = group_sizes(ends, frame_rows)
+    counts = jnp.stack([1.0 / jnp.maximum(jnp.sum(live), 1.0), live_count])
     kernel_part = 0.0
     norm_part = 0.0
     for ascent_step in range(ASCENT):
@@ -456,32 +520,11 @@
         glu = (value_half * gate_half * live).astype(jnp.bfloat16)
         padded = with_halo(glu, half_span)
         conv_out = conv(padded, kernel, frame_rows, False)
-        local_sum = jnp.sum(live * conv_out, axis=0)
-        apart = conv_out - local_sum / jnp.maximum(jnp.sum(live), 1.0)
-        total, spread = sum_everywhere(
-            local_sum, jnp.sum(live * apart * apart, axis=0), sizes, True, 1 + 2 * ascent_step
-        )
-        centred = conv_out - total / live_count
-        variance = spread / live_count
-        inv_std = lax.rsqrt(variance + batch_epsilon)
-        scaled = centred * inv_std
-        pre_act = bn_gain * scaled + bn_shift
-        pre_sigmoid = jax.nn.sigmoid(pre_act)
-        grad_pre = upstream * pre_sigmoid * (1.0 + pre_act * (1.0 - pre_sigmoid))
-        both = jnp.stack(
-            sum_everywhere(
-                jnp.sum(grad_pre * scaled, axis=0),
-                jnp.sum(grad_pre, axis=0),
-                sizes,
-                False,
-                2 + 2 * ascent_step,
-            )
+        grad_conv, both, taps = batch_norm(
+            sizes, counts, conv_out, upstream, live, padded, bn_gain, bn_shift, 1 + ascent_step
         )
         norm_part = norm_part + both
-        grad_conv = (
-            live * inv_std * bn_gain * (grad_pre - (both[1] + scaled * both[0]) / live_count)
-        ).astype(jnp.bfloat16)
-        kernel_part = kernel_part + tap_grad(grad_conv.astype(jnp.float32), padded, tap_count)
+        kernel_part = kernel_part + taps
         if ascent_step + 1 < ASCENT:
             grad_pad = with_halo(grad_conv, half_span)
             grad_glu = (conv(grad_pad, kernel, frame_rows, True) * live).astype(jnp.bfloat16)
@@ -508,7 +551,7 @@
                 / (jnp.sqrt(square_total) + ascent_epsilon)
             )
     width = model_width // lax.axis_size("tm")
-    by_shard = kernel_part.reshape(tap_count, 16, 2, 2, width).transpose(3, 1, 2, 0, 4)
+    by_shard = kernel_part[:tap_count].reshape(tap_count, 16, 2, 2, width).transpose(3, 1, 2, 0, 4)
     by_shard = by_shard.reshape(64, tap_count * width)
     by_shard = jnp.pad(by_shard, ((0, 0), (0, 1024 - tap_count * width)))
     kernel_total = scatter_taps(by_shard.reshape(2, 16, 2, 8, 128), 6).reshape(-1)

time: 363 us -> 305 us (0.84)
  local copies, waits for them, and re-layouts: 46.8 us -> 10 us
  other arithmetic: 42.9 us -> 26.5 us
  Pallas kernels: 230 us -> 223 us
  waiting for transfers between devices: 3.44 us -> 8.87 us
    reduce_sum x13 -> x1, other arithmetic: 21.8 us -> 0.1 us  [group_sizes(): sizes = jnp.stack([here, jnp.pad(jnp.sum(live, axis=1), (0, 16))])]
    another operation x77 -> x1, local copies, waits for them, and re-layouts: 21.2 us -> 0.01 us  [group_sizes(): sizes = jnp.stack([here, jnp.pad(jnp.sum(live, axis=1), (0, 16))])]
    unnamed x215 -> x29, local copies, waits for them, and re-layouts: 19 us -> 1.5 us
    add x0 -> x3, other arithmetic: none -> 8.58 us  [the longest x2 7.63 us: conv(): result = term if result is None else result + term]
    ppermute x3, waiting for transfers between devices: 3.44 us -> 8.86 us  [with_halo(): lax.ppermute(block[:half_span], 'tm', [(i + 1, i) for i in range(count -...]
    pallas_call x1, Pallas kernels: 22 us -> 18.3 us  [square_sum(): pl.pallas_call(square_sum_kernel, out_shape=jax.ShapeDtypeStruct((8, 128)...]
    pallas_call x4 -> x2, Pallas kernels: 114 us -> 114 us  [batch_norm(): pl.pallas_call(batch_norm_kernel, out_shape=(jax.ShapeDtypeStruct((rows,...]
  transfers between devices with their start and end apart: 6 -> 6, of which waited for: 1 -> 2; matrix products, arithmetic and copies ran while one was open for 6% -> 1% of each run, Pallas kernels for 0% -> 0%
where the time goes in v4:
time: 305 us; the launch traced here: 303 us
  Pallas kernels  223 us (73%)
  other arithmetic  26.5 us (9%)
  starting transfers between devices  15.8 us (5%)
  matrix products  15.3 us (5%)
  local copies, waits for them, and re-layouts  10 us (3%)
  waiting for transfers between devices  8.87 us (3%)
  between operations  3.85 us (1%)
    pallas_call x2, Pallas kernels, batch_norm(): pl.pallas_call(batch_norm_kernel, out_shape=(jax.ShapeDtypeStruct((rows,...  114 us
    pallas_call x1, Pallas kernels, gather(): pl.pallas_call(gather_kernel, out_shape=jax.ShapeDtypeStruct((16, 2, 2, s...  67.8 us
    pallas_call x1, Pallas kernels, scatter_taps(): pl.pallas_call(scatter_taps_kernel, out_shape=jax.ShapeDtypeStruct((8, 12...  23.3 us
    pallas_call x1, Pallas kernels, square_sum(): pl.pallas_call(square_sum_kernel, out_shape=jax.ShapeDtypeStruct((8, 128)...  18.3 us
    dot_general x2, matrix products, on_device(): lax.dot_general(normed.astype(jnp.bfloat16), weight_full, (((1,), (1,)),...  13.8 us
    ppermute x3, starting transfers between devices, with_halo(): lax.ppermute(block[-half_span:], 'tm', [(i, i + 1) for i in range(count -...  9.65 us
    ppermute x3, waiting for transfers between devices, with_halo(): lax.ppermute(block[:half_span], 'tm', [(i + 1, i) for i in range(count -...  8.86 us
    add x2, other arithmetic, conv(): result = term if result is None else result + term  7.63 us
  transfers between devices with their start and end apart: 6, of which 2 were waited for; matrix products, arithmetic and copies ran while one was open for 1% of the time, Pallas kernels for 0%

profile of v4, /device:TPU:1, one launch (start us, length us, event | category | flops | bytes accessed | tf_op | source)
XLA Modules:
  0.0 303.4 jit_solution(4341037075379519714)
XLA Ops:
  2.5 1.4 fusion.118
  3.9 1.4 multiply_reduce_fusion.2
  6.0 67.8 %shard_map.103 = bf16[16,2,2,6,8,1536]{5,4,3,2,1,0:T(8,128)(2,1)} custom-call(bf16[6,8,1536]{2,1,0:T(8,128)(2,1)} %bitcast.83), custom_call_target="tpu_custom_call" | custom-call | tf_op jit(solution)/shard_map/pallas_call | solution.py:463
  73.9 7.0 %fusion.122 = f32[128,3072]{1,0:T(8,128)S(1)} fusion(bf16[3072,1536]{1,0:T(8,128)(2,1)} %bitcast.76, bf16[1,128,1536]{2,1,0:T(8,128)(2,1)S(1)} %copy-done.2, bf16[1,128,1536]{2,1,0:T(8,128)(2,1)S(1)} %copy-done.3, f32[128]{0:T(128)S(1)} %get-tuple-element.78, f32[128]{0:T(128)S(1)} %broadcast_multiply_fusion.3, f32[128]{0:T(128)S(1)} %broadcast_select_fusion.1), kind=kOutput, calls=%fused_computation.234 | convolution fusion | flops 1209335808 | bytes 11798016 | tf_op jit(solution)/shard_map/dot_general | solution.py:512
  82.1 2.7 collective-permute-start
  84.8 1.9 collective-permute-start.1
  92.7 3.8 %fusion.78.conv_ref = f32[128,1536]{1,0:T(8,128)} fusion(f32[158,1536]{1,0:T(8,128)S(1)} %maximum_convert_fusion.padded_ref, f32[1536]{0:T(1024)S(1)} %get-tuple-element.56, f32[1536]{0:T(1024)S(1)} %get-tuple-element.57, f32[1536]{0:T(1024)S(1)} %get-tuple-element.28, f32[1536]{0:T(1024)S(1)} %get-tuple-element.29, f32[1536]{0:T(1024)S(1)} %get-tuple-element.30, ...), kind=kLoop, calls=%fused_computation.148 | loop fusion | flops 11993088 | bytes 25356288 | tf_op jit(solution)/shard_map/add | solution.py:485
  97.2 59.7 %shard_map.104 = (bf16[128,1536]{1,0:T(8,128)(2,1)}, f32[2,1536]{1,0:T(2,128)}, f32[32,1536]{1,0:T(8,128)}) custom-call(f32[2,3,32]{2,1,0:T(4,128)} %pad_maximum_fusion.sizes, f32[2]{0:T(128)} %pad_maximum_fusion.3.counts, f32[128,1536]{1,0:T(8,128)} %fusion.78.conv_ref, f32[128,1536]{1,0:T(8,128)} %get-tuple-element.80.up_ref, ...), custom_call_target="tpu_custom_call" | custom-call | tf_op jit(solution)/shard_map/pallas_call | solution.py:208
  157.8 3.5 %collective-permute-start.2 = (bf16[15,1536]{1,0:T(8,128)(2,1)S(1)}, bf16[15,1536]{1,0:T(8,128)(2,1)S(1)}, u32[]{:S(2)}, u32[]{:S(2)}) collective-permute-start(bf16[15,1536]{1,0:T(8,128)(2,1)S(1)} %get-tuple-element.71), channel_id=1, source_target_pairs={{0,1},{1,2},{2,3},{3,4},{4,5},{5,6},{6,7},{7,8},{8,9},{9,10},{10,1... | collective-permute-start | bytes 138248 | tf_op jit(solution)/shard_map/ppermute | solution.py:25
  161.3 2.1 collective-permute-start.3
  164.1 4.1 %collective-permute-done.3 = bf16[15,1536]{1,0:T(8,128)(2,1)S(1)} collective-permute-done((bf16[15,1536]{1,0:T(8,128)(2,1)S(1)}, bf16[15,1536]{1,0:T(8,128)(2,1)S(1)}, u32[]{:S(2)}, u32[]{:S(2)}) %collective-permute-start.3) | collective-permute-done | bytes 46112 | tf_op jit(solution)/shard_map/ppermute | solution.py:26
  169.5 3.3 %fusion.2 = (bf16[128,1536]{1,0:T(8,128)(2,1)S(1)}, bf16[128,1536]{1,0:T(8,128)(2,1)S(1)}) fusion(f32[128,3072]{1,0:T(8,128)S(1)} %fusion.122, f32[128]{0:T(128)S(1)} %get-tuple-element.64, f32[158,1536]{1,0:T(8,128)S(1)} %maximum_convert_fusion.1, f32[1536]{0:T(1024)S(1)} %get-tuple-element.56, f32[1536]{0:T(1024)S(1)} %get-tuple-element.57, ...), kind=kLoop, calls=%fused_computation.8 | loop fusion | flops 13565952 | bytes 26143232 | tf_op jit(solution)/shard_map/convert.3
  173.1 1.5 fusion.133
  175.8 18.3 %shard_map.105 = f32[8,128]{1,0:T(8,128)} custom-call(f32[8,128]{1,0:T(8,128)} %get-tuple-element.60.x_ref), custom_call_target="tpu_custom_call" | custom-call | tf_op jit(solution)/shard_map/pallas_call | solution.py:254
  194.1 1.3 reduce_sum.117
  197.5 6.8 %fusion.120 = f32[128,3072]{1,0:T(8,128)S(1)} fusion(bf16[3072,1536]{1,0:T(8,128)(2,1)} %bitcast.77, f32[128,1536]{1,0:T(8,128)S(1)} %get-tuple-element.59, f32[128]{0:T(128)S(1)} %add_rsqrt_fusion, f32[128]{0:T(128)S(1)} %broadcast_multiply_fusion), kind=kOutput, calls=%fused_computation.232 | convolution fusion | flops 1208549376 | bytes 11797504 | tf_op jit(solution)/shard_map/dot_general | solution.py:512
  204.6 3.4 %collective-permute-start.4 = (bf16[15,1536]{1,0:T(8,128)(2,1)S(1)}, bf16[15,1536]{1,0:T(8,128)(2,1)S(1)}, u32[]{:S(2)}, u32[]{:S(2)}) collective-permute-start(bf16[15,1536]{1,0:T(8,128)(2,1)S(1)} %get-tuple-element.69), channel_id=1, source_target_pairs={{0,1},{1,2},{2,3},{3,4},{4,5},{5,6},{6,7},{7,8},{8,9},{9,10},{10,1... | collective-permute-start | bytes 138248 | tf_op jit(solution)/shard_map/ppermute | solution.py:25
  208.0 2.1 collective-permute-start.5
  210.2 4.8 %collective-permute-done.5 = bf16[15,1536]{1,0:T(8,128)(2,1)S(1)} collective-permute-done((bf16[15,1536]{1,0:T(8,128)(2,1)S(1)}, bf16[15,1536]{1,0:T(8,128)(2,1)S(1)}, u32[]{:S(2)}, u32[]{:S(2)}) %collective-permute-start.5) | collective-permute-done | bytes 46112 | tf_op jit(solution)/shard_map/ppermute | solution.py:26
  215.1 3.8 %fusion.11.conv_ref = f32[128,1536]{1,0:T(8,128)} fusion(f32[158,1536]{1,0:T(8,128)S(1)} %maximum_convert_fusion.2.padded_ref, f32[1536]{0:T(1024)S(1)} %get-tuple-element.56, f32[1536]{0:T(1024)S(1)} %get-tuple-element.57, f32[1536]{0:T(1024)S(1)} %get-tuple-element.28, f32[1536]{0:T(1024)S(1)} %get-tuple-element.29, f32[1536]{0:T(1024)S(1)} %get-tuple-element.30, ...), kind=kLoop, calls=%fused_computation.18 | loop fusion | flops 11993088 | bytes 25356288 | tf_op jit(solution)/shard_map/add | solution.py:485
  218.9 53.9 %shard_map.106 = (bf16[128,1536]{1,0:T(8,128)(2,1)}, f32[2,1536]{1,0:T(2,128)}, f32[32,1536]{1,0:T(8,128)}) custom-call(f32[2,3,32]{2,1,0:T(4,128)} %pad_maximum_fusion.sizes, f32[2]{0:T(128)} %pad_maximum_fusion.3.counts, f32[128,1536]{1,0:T(8,128)} %fusion.11.conv_ref, f32[128,1536]{1,0:T(8,128)} %get-tuple-element.80.up_ref, ...), custom_call_target="tpu_custom_call" | custom-call | tf_op jit(solution)/shard_map/pallas_call | solution.py:208
  273.8 1.7 reshape.193
  277.4 23.3 %shard_map.107 = f32[8,128]{1,0:T(8,128)} custom-call(f32[2,16,2,8,128]{4,3,2,1,0:T(8,128)} %bitcast.82), custom_call_target="tpu_custom_call" | custom-call | tf_op jit(solution)/shard_map/pallas_call | solution.py:283
  302.1 1.3 dynamic-slice_add_fusion
  (80 shorter events, 18.6 us)
Async XLA Ops:
  6.0 67.8 %copy-start.2 = (bf16[1,128,1536]{2,1,0:T(8,128)(2,1)S(1)}, bf16[1,128,1536]{2,1,0:T(8,128)(2,1)}, u32[]{:S(2)}) copy-start(bf16[1,128,1536]{2,1,0:T(8,128)(2,1)} %param.9) | copy-start | bytes 1179652
  6.0 67.9 %copy-start.3 = (bf16[1,128,1536]{2,1,0:T(8,128)(2,1)S(1)}, bf16[1,128,1536]{2,1,0:T(8,128)(2,1)}, u32[]{:S(2)}) copy-start(bf16[1,128,1536]{2,1,0:T(8,128)(2,1)} %param.8) | copy-start | bytes 1179652
  73.9 7.0 %copy-start.4 = (bf16[1,128,1536]{2,1,0:T(8,128)(2,1)S(1)}, bf16[1,128,1536]{2,1,0:T(8,128)(2,1)}, u32[]{:S(2)}) copy-start(bf16[1,128,1536]{2,1,0:T(8,128)(2,1)} %param.10) | copy-start | bytes 1179652
  80.9 5.9 %copy-start.9 = (s32[8]{0:T(128)S(1)}, s32[8]{0:T(128)}, u32[]{:S(2)}) copy-start(s32[8]{0:T(128)} %param.15) | copy-start | bytes 100
  80.9 6.6 %copy-start.6 = (f32[31,1536]{1,0:T(8,128)S(1)}, f32[31,1536]{1,0:T(8,128)}, u32[]{:S(2)}) copy-start(f32[31,1536]{1,0:T(8,128)} %param.12) | copy-start | bytes 571396
  80.9 10.5 %copy-start.7 = (f32[1536]{0:T(1024)S(1)}, f32[1536]{0:T(1024)}, u32[]{:S(2)}) copy-start(f32[1536]{0:T(1024)} %param.13) | copy-start | bytes 18436
  80.9 11.1 %copy-start.8 = (f32[1536]{0:T(1024)S(1)}, f32[1536]{0:T(1024)}, u32[]{:S(2)}) copy-start(f32[1536]{0:T(1024)} %param.14) | copy-start | bytes 18436
  82.1 10.5 %collective-permute-start = (bf16[15,1536]{1,0:T(8,128)(2,1)S(1)}, bf16[15,1536]{1,0:T(8,128)(2,1)S(1)}, u32[]{:S(2)}, u32[]{:S(2)}) collective-permute-start(bf16[15,1536]{1,0:T(8,128)(2,1)S(1)} %get-tuple-element.73), channel_id=1, source_target_pairs={{0,1},{1,2},{2,3},{3,4},{4,5},{5,6},{6,7},{7,8},{8,9},{9,10},{10,1... | collective-permute-start | bytes 138248 | tf_op jit(solution)/shard_map/ppermute | solution.py:25
  84.8 7.8 %collective-permute-start.1 = (bf16[15,1536]{1,0:T(8,128)(2,1)S(1)}, bf16[15,1536]{1,0:T(8,128)(2,1)S(1)}, u32[]{:S(2)}, u32[]{:S(2)}) collective-permute-start(bf16[15,1536]{1,0:T(8,128)(2,1)S(1)} %get-tuple-element.74), channel_id=1, source_target_pairs={{1,0},{2,1},{3,2},{4,3},{5,4},{6,5},{7,6},{8,7},{9,8},{10,9},{11,1... | collective-permute-start | bytes 138248 | tf_op jit(solution)/shard_map/ppermute | solution.py:26
  92.7 3.8 %copy-start.1 = (f32[158,1536]{1,0:T(8,128)}, f32[158,1536]{1,0:T(8,128)S(1)}, u32[]{:S(2)}) copy-start(f32[158,1536]{1,0:T(8,128)S(1)} %maximum_convert_fusion.padded_ref) | copy-start | bytes 2912260
  157.8 6.3 %collective-permute-start.2 = (bf16[15,1536]{1,0:T(8,128)(2,1)S(1)}, bf16[15,1536]{1,0:T(8,128)(2,1)S(1)}, u32[]{:S(2)}, u32[]{:S(2)}) collective-permute-start(bf16[15,1536]{1,0:T(8,128)(2,1)S(1)} %get-tuple-element.71), channel_id=1, source_target_pairs={{0,1},{1,2},{2,3},{3,4},{4,5},{5,6},{6,7},{7,8},{8,9},{9,10},{10,1... | collective-permute-start | bytes 138248 | tf_op jit(solution)/shard_map/ppermute | solution.py:25
  161.3 6.9 %collective-permute-start.3 = (bf16[15,1536]{1,0:T(8,128)(2,1)S(1)}, bf16[15,1536]{1,0:T(8,128)(2,1)S(1)}, u32[]{:S(2)}, u32[]{:S(2)}) collective-permute-start(bf16[15,1536]{1,0:T(8,128)(2,1)S(1)} %get-tuple-element.72), channel_id=1, source_target_pairs={{1,0},{2,1},{3,2},{4,3},{5,4},{6,5},{7,6},{8,7},{9,8},{10,9},{11,1... | collective-permute-start | bytes 138248 | tf_op jit(solution)/shard_map/ppermute | solution.py:26
  168.2 4.8 %slice-start = ((s8[9437184]{0:T(1024)(128)(4,1)}), s8[4194304]{0:T(1024)(128)(4,1)S(1)}, s32[]{:S(2)}) async-start(s8[9437184]{0:T(1024)(128)(4,1)} %bitcast.78), calls=%async_computation | async-start | bytes 8388608
  169.5 3.6 %slice-start.1 = ((s8[9437184]{0:T(1024)(128)(4,1)}), s8[4194304]{0:T(1024)(128)(4,1)S(1)}, s32[]{:S(2)}) async-start(s8[9437184]{0:T(1024)(128)(4,1)} %bitcast.78), calls=%async_computation.1 | async-start | bytes 8388608
  169.5 3.6 %slice-start.2 = ((s8[9437184]{0:T(1024)(128)(4,1)}), s8[1048576]{0:T(1024)(128)(4,1)S(1)}, s32[]{:S(2)}) async-start(s8[9437184]{0:T(1024)(128)(4,1)} %bitcast.78), calls=%async_computation.2 | async-start | bytes 2097152
  204.6 5.6 %collective-permute-start.4 = (bf16[15,1536]{1,0:T(8,128)(2,1)S(1)}, bf16[15,1536]{1,0:T(8,128)(2,1)S(1)}, u32[]{:S(2)}, u32[]{:S(2)}) collective-permute-start(bf16[15,1536]{1,0:T(8,128)(2,1)S(1)} %get-tuple-element.69), channel_id=1, source_target_pairs={{0,1},{1,2},{2,3},{3,4},{4,5},{5,6},{6,7},{7,8},{8,9},{9,10},{10,1... | collective-permute-start | bytes 138248 | tf_op jit(solution)/shard_map/ppermute | solution.py:25
  208.0 6.9 %collective-permute-start.5 = (bf16[15,1536]{1,0:T(8,128)(2,1)S(1)}, bf16[15,1536]{1,0:T(8,128)(2,1)S(1)}, u32[]{:S(2)}, u32[]{:S(2)}) collective-permute-start(bf16[15,1536]{1,0:T(8,128)(2,1)S(1)} %get-tuple-element.70), channel_id=1, source_target_pairs={{1,0},{2,1},{3,2},{4,3},{5,4},{6,5},{7,6},{8,7},{9,8},{10,9},{11,1... | collective-permute-start | bytes 138248 | tf_op jit(solution)/shard_map/ppermute | solution.py:26
  215.1 3.8 %copy-start = (f32[158,1536]{1,0:T(8,128)}, f32[158,1536]{1,0:T(8,128)S(1)}, u32[]{:S(2)}) copy-start(f32[158,1536]{1,0:T(8,128)S(1)} %maximum_convert_fusion.2.padded_ref) | copy-start | bytes 2912260
  218.9 53.9 %copy-start.5 = (f32[32,1536]{1,0:T(8,128)S(1)}, f32[32,1536]{1,0:T(8,128)}, u32[]{:S(2)}) copy-start(f32[32,1536]{1,0:T(8,128)} %get-tuple-element.9) | copy-start | bytes 589828

commit v5 on v4

--- a/solution.py
+++ b/solution.py
@@ -18,13 +18,6 @@
     centre = summed - jnp.mean(summed, axis=-1, keepdims=True)
     inverse = lax.rsqrt(jnp.mean(centre * centre, axis=-1, keepdims=True) + layer_epsilon)
     return (centre * inverse, inverse)
-
-
-def with_halo(block, half_span):
-    count = lax.axis_size("tm")
-    before = lax.ppermute(block[-half_span:], "tm", [(i, i + 1) for i in range(count - 1)])
-    after = lax.ppermute(block[:half_span], "tm", [(i + 1, i) for i in range(count - 1)])
-    return jnp.concatenate([before, block, after], axis=0).astype(jnp.float32)
 
 
 def place():
@@ -133,15 +126,22 @@
     exchange(plane, lambda peer: b3.at[me], b3, sems.at[2])
 
 
-def batch_norm_kernel(
-    sizes, counts, conv_ref, up_ref, live_ref, padded_ref, gain_ref, shift_ref,
-    grad_ref, both_ref, taps_ref,
-    scaled_ref, pre_ref, inv_ref, s1, a1, a2, a3, s2, c1, c2, c3, sems1, sems2,
+def neighbours():
+    dp, tm = lax.axis_index("dp"), lax.axis_index("tm")
+    return (3, 0, lambda i: (dp, lax.rem(tm + 1 + (i - 1) * 62, 64)))
+
+
+def conv_kernel(
+    back, sizes, counts, glu_ref, up_ref, live_ref, kernel_ref, gain_ref, shift_ref,
+    both_ref, taps_ref, grad_glu_ref,
+    padded, conv_ref, scaled_ref, pre_ref, inv_ref, grad_ref, halo1, halo2,
+    s1, a1, a2, a3, s2, c1, c2, c3, sems1, sems2, halo_sems,
 ):
-    meet(flat_plane(), groups()[2])
-    tiles = conv_ref.shape[1] // 128
-    rows = conv_ref.shape[0]
+    meet(flat_plane(), groups()[2], neighbours())
+    tm = lax.axis_index("tm")
+    rows, width = glu_ref.shape
     total_live = counts[1]
+    beside = neighbours()[2]
 
     def at(i):
         return pl.ds(pl.multiple_of(i * 128, 128), 128)
@@ -151,13 +151,51 @@
             body(i)
             return carry
 
-        lax.fori_loop(0, tiles, step, 0)
-
+        lax.fori_loop(0, width // 128, step, 0)
+
+    def halo_copies(block, halo, base):
+        return [
+            pltpu.make_async_remote_copy(
+                src_ref=block.at[pl.ds((rows - 16) * (1 - side), 16)],
+                dst_ref=halo.at[side],
+                send_sem=halo_sems.at[0, base + side],
+                recv_sem=halo_sems.at[1, base + side],
+                device_id=beside(1 + side),
+                device_id_type=pl.DeviceIdType.MESH,
+            )
+            for side in (0, 1)
+        ]
+
+    def fill(block, halo):
+        first = jnp.where(tm > 0, 1.0, 0.0).astype(jnp.float32)
+        last = jnp.where(tm < 63, 1.0, 0.0).astype(jnp.float32)
+
+        def tile(i):
+            padded[pl.ds(0, 16), at(i)] = halo[0, :, at(i)].astype(jnp.float32) * first
+            padded[pl.ds(16, rows), at(i)] = block[:, at(i)].astype(jnp.float32)
+            padded[pl.ds(rows + 16, 16), at(i)] = halo[1, :, at(i)].astype(jnp.float32) * last
+
+        each(tile)
+
+    def convolve(i, start_of):
+        total = None
+        for j in range(31):
+            term = kernel_ref[pl.ds(j, 1), at(i)] * padded[pl.ds(start_of(j), rows), at(i)]
+            total = term if total is None else total + term
+        return total
+
+    first_halo = halo_copies(glu_ref, halo1, 0)
+    for copy in first_halo:
+        copy.start()
     s1[...] = jnp.zeros(s1.shape, jnp.float32)
     s2[...] = jnp.zeros(s2.shape, jnp.float32)
+    for copy in first_halo:
+        copy.wait()
+    fill(glu_ref, halo1)
 
     def moments(i):
-        part, live = conv_ref[:, at(i)], live_ref[...]
+        part, live = convolve(i, lambda j: j + 1), live_ref[...]
+        conv_ref[:, at(i)] = part
         local = jnp.sum(part * live, axis=0, keepdims=True)
         apart = part - local * counts[0]
         s1[i, 0:1] = local
@@ -190,41 +228,74 @@
             live_ref[...]
             * (inv_ref[:, at(i)] * gain_ref[:, at(i)])
             * (grad_pre - (found[1:2] + scaled * found[0:1]) / total_live)
-        ).astype(jnp.bfloat16)
-        grad_ref[:, at(i)] = grad
-        grad = grad.astype(jnp.float32)
+        )
+        grad_ref[:, at(i)] = grad.astype(jnp.bfloat16)
+
+    each(backward)
+    if back:
+        second_halo = halo_copies(grad_ref, halo2, 2)
+        for copy in second_halo:
+            copy.start()
+
+    def tap_sums(i):
+        grad = grad_ref[:, at(i)].astype(jnp.float32)
         for j in range(31):
-            window = padded_ref[pl.ds(j, rows), at(i)]
+            window = padded[pl.ds(j + 1, rows), at(i)]
             taps_ref[pl.ds(j, 1), at(i)] = jnp.sum(grad * window, axis=0, keepdims=True)
         taps_ref[pl.ds(31, 1), at(i)] = jnp.zeros((1, 128), jnp.float32)
 
-    each(backward)
-
-
-def batch_norm(sizes, counts, conv_out, upstream, live, padded, gain, shift, number):
-    rows, width = conv_out.shape
+    each(tap_sums)
+    if back:
+        for copy in second_halo:
+            copy.wait()
+        fill(grad_ref, halo2)
+
+        def input_grad(i):
+            part = convolve(i, lambda j: 31 - j) * live_ref[...]
+            grad_glu_ref[:, at(i)] = part.astype(jnp.bfloat16)
+
+        each(input_grad)
+
+
+def conv_step(sizes, counts, glu, upstream, live, kernel, gain, shift, back, number):
+    rows, width = glu.shape
     smem, vmem = pl.BlockSpec(memory_space=pltpu.SMEM), pl.BlockSpec(memory_space=pltpu.VMEM)
     slots = [pltpu.VMEM((n, 2, 128), jnp.float32) for n in (32, 32, 16, 32)]
+    whole = pltpu.VMEM((rows, width), jnp.float32)
+    halo = pltpu.VMEM((2, 16, width), jnp.bfloat16)
+    shapes = [
+        jax.ShapeDtypeStruct((2, width), jnp.float32),
+        jax.ShapeDtypeStruct((32, width), jnp.float32),
+    ]
+    if back:
+        shapes.append(jax.ShapeDtypeStruct((rows, width), jnp.bfloat16))
+
+    def body(*refs):
+        refs = list(refs) if back else list(refs[:10]) + [None] + list(refs[10:])
+        conv_kernel(back, *refs)
+
     return pl.pallas_call(
-        batch_norm_kernel,
-        out_shape=(
-            jax.ShapeDtypeStruct((rows, width), jnp.bfloat16),
-            jax.ShapeDtypeStruct((2, width), jnp.float32),
-            jax.ShapeDtypeStruct((32, width), jnp.float32),
-        ),
+        body,
+        out_shape=shapes,
         in_specs=[smem, smem] + [vmem] * 6,
-        out_specs=(vmem, vmem, vmem),
+        out_specs=[vmem] * len(shapes),
         scratch_shapes=[
-            pltpu.VMEM((rows, width), jnp.float32),
-            pltpu.VMEM((rows, width), jnp.float32),
+            pltpu.VMEM((rows + 32, width), jnp.float32),
+            whole,
+            whole,
+            whole,
             pltpu.VMEM((1, width), jnp.float32),
+            pltpu.VMEM((rows, width), jnp.bfloat16),
+            halo,
+            halo,
         ]
         + slots
         + slots
-        + [pltpu.SemaphoreType.DMA((3, 2, 32)), pltpu.SemaphoreType.DMA((3, 2, 32))],
+        + [pltpu.SemaphoreType.DMA((3, 2, 32)), pltpu.SemaphoreType.DMA((3, 2, 32))]
+        + [pltpu.SemaphoreType.DMA((2, 4))],
         compiler_params=pltpu.CompilerParams(collective_id=number, has_side_effects=True),
-    )(sizes, counts, conv_out, upstream, jnp.broadcast_to(live, (rows, 128)), padded,
-      gain[None], shift[None])
+    )(sizes, counts, glu, upstream, jnp.broadcast_to(live, (rows, 128)),
+      jnp.pad(kernel, ((0, 1), (0, 0))), gain[None], shift[None])
 
 
 def group_sizes(ends, frame_rows):
@@ -253,12 +324,12 @@
 def square_sum(rows, number):
     return pl.pallas_call(
         square_sum_kernel,
-        out_shape=jax.ShapeDtypeStruct((8, 128), jnp.float32),
+        out_shape=jax.ShapeDtypeStruct((1, 128), jnp.float32),
         in_specs=[pl.BlockSpec(memory_space=pltpu.VMEM)],
         out_specs=pl.BlockSpec(memory_space=pltpu.VMEM),
         scratch_shapes=[
-            pltpu.VMEM((16, 8, 128), jnp.float32),
-            pltpu.VMEM((4, 8, 128), jnp.float32),
+            pltpu.VMEM((16, 1, 128), jnp.float32),
+            pltpu.VMEM((4, 1, 128), jnp.float32),
             pltpu.SemaphoreType.DMA((2, 2, 16)),
         ],
         compiler_params=pltpu.CompilerParams(collective_id=number, has_side_effects=True),
@@ -476,21 +547,10 @@
     return out.reshape(-1, weight.shape[1])
 
 
-def conv(padded, kernel, out_length, flip):
-    taps = kernel.shape[0]
-    result = None
-    for offset in range(taps):
-        start = taps - 1 - offset if flip else offset
-        term = kernel[offset] * padded[start : start + out_length]
-        result = term if result is None else result + term
-    return result
-
-
 def on_device(features, start_noise, cotangent, in_weight, kernel, bn_gain, bn_shift, ends):
     frame_rows = features.shape[1]
     model_width = features.shape[2]
     tap_count = kernel.shape[0]
-    half_span = (tap_count - 1) // 2
     shard_index = lax.axis_index("tm")
     group_index = lax.axis_index("dp")
     utter_end = lax.dynamic_index_in_dim(ends, group_index, 0, keepdims=False)
@@ -518,16 +578,14 @@
         value_half = hidden[:, :model_width]
         gate_half = jax.nn.sigmoid(hidden[:, model_width:])
         glu = (value_half * gate_half * live).astype(jnp.bfloat16)
-        padded = with_halo(glu, half_span)
-        conv_out = conv(padded, kernel, frame_rows, False)
-        grad_conv, both, taps = batch_norm(
-            sizes, counts, conv_out, upstream, live, padded, bn_gain, bn_shift, 1 + ascent_step
+        back = ascent_step + 1 < ASCENT
+        both, taps, *rest = conv_step(
+            sizes, counts, glu, upstream, live, kernel, bn_gain, bn_shift, back, 1 + ascent_step
         )
         norm_part = norm_part + both
         kernel_part = kernel_part + taps
-        if ascent_step + 1 < ASCENT:
-            grad_pad = with_halo(grad_conv, half_span)
-            grad_glu = (conv(grad_pad, kernel, frame_rows, True) * live).astype(jnp.bfloat16)
+        if back:
+            grad_glu = rest[0]
             grad_float = grad_glu.astype(jnp.float32)
             grad_hidden = jnp.concatenate(
                 [grad_float * gate_half, grad_float * value_half * gate_half * (1.0 - gate_half)],
@@ -543,7 +601,7 @@
                     - normed * jnp.mean(grad_normed * normed, axis=-1, keepdims=True)
                 )
             )
-            squares = jnp.sum((direction * direction).reshape(16, 8, 12, 128), axis=(0, 2))
+            squares = jnp.sum((direction * direction).reshape(128, 12, 128), axis=(0, 1))[None]
             square_total = jnp.sum(square_sum(squares, 5))
             perturbation = perturbation + direction * (
                 ascent_rate

time: 305 us -> 290 us (0.951)
  starting transfers between devices: 15.8 us -> 0 us
  Pallas kernels: 223 us -> 236 us
  other arithmetic: 26.5 us -> 16.5 us
  waiting for transfers between devices: 8.87 us -> 0 us
  matrix products: 15.3 us -> 19 us
    ppermute x6 -> x0, starting transfers between devices: 15.8 us -> none  [the longest x3 9.65 us: with_halo(): lax.ppermute(block[-half_span:], 'tm', [(i, i + 1) for i in range(count -...]
    pallas_call x3, Pallas kernels: 132 us -> 147 us  [the longest x2 129 us: conv_step(): pl.pallas_call(body, out_shape=shapes, in_specs=[smem, smem] + [vmem] * 6...]
    ppermute x6 -> x0, waiting for transfers between devices: 8.87 us -> none  [the longest x3 8.86 us: with_halo(): lax.ppermute(block[:half_span], 'tm', [(i + 1, i) for i in range(count -...]
    add x2 -> x0, other arithmetic: 7.63 us -> none  [conv(): result = term if result is None else result + term]
    dot_general x1, matrix products: 1.51 us -> 5.28 us  [on_device(): jnp.dot(grad_hidden, weight_full, preferred_element_type=jnp.float32)]
  transfers between devices with their start and end apart: 6 -> 0, of which waited for: 2 -> 0; matrix products, arithmetic and copies ran while one was open for 1% -> 0% of each run, Pallas kernels for 0% -> 0%
where the time goes in v5:
time: 290 us; the launch traced here: 288 us
  Pallas kernels  236 us (81%)
  matrix products  19 us (7%)
  other arithmetic  16.5 us (6%)
  local copies, waits for them, and re-layouts  12.4 us (4%)
  between operations  3.63 us (1%)
    pallas_call x2, Pallas kernels, conv_step(): pl.pallas_call(body, out_shape=shapes, in_specs=[smem, smem] + [vmem] * 6...  129 us
    pallas_call x1, Pallas kernels, gather(): pl.pallas_call(gather_kernel, out_shape=jax.ShapeDtypeStruct((16, 2, 2, s...  67.8 us
    pallas_call x1, Pallas kernels, scatter_taps(): pl.pallas_call(scatter_taps_kernel, out_shape=jax.ShapeDtypeStruct((8, 12...  21.8 us
    pallas_call x1, Pallas kernels, square_sum(): pl.pallas_call(square_sum_kernel, out_shape=jax.ShapeDtypeStruct((1, 128)...  17.6 us
    dot_general x2, matrix products, on_device(): lax.dot_general(normed.astype(jnp.bfloat16), weight_full, (((1,), (1,)),...  13.7 us

profile of v5, /device:TPU:1, one launch (start us, length us, event | category | flops | bytes accessed | tf_op | source)
XLA Modules:
  0.0 287.9 jit_solution(11336161082508964500)
XLA Ops:
  0.7 1.3 dynamic_slice.11
  2.7 1.3 reduce_sum.120
  5.3 1.4 fusion.26
  6.7 1.4 multiply_reduce_fusion.3
  11.0 1.3 broadcast_in_dim.13.refs_6_
  12.3 1.3 broadcast_in_dim.14.refs_7_
  15.6 1.6 pad.14.refs_5_
  17.2 67.8 %shard_map.103 = bf16[16,2,2,6,8,1536]{5,4,3,2,1,0:T(8,128)(2,1)} custom-call(bf16[6,8,1536]{2,1,0:T(8,128)(2,1)} %bitcast.82), custom_call_target="tpu_custom_call" | custom-call | tf_op jit(solution)/shard_map/pallas_call | solution.py:534
  85.1 6.9 %fusion.30 = f32[128,3072]{1,0:T(8,128)S(1)} fusion(bf16[3072,1536]{1,0:T(8,128)(2,1)} %bitcast.77, bf16[1,128,1536]{2,1,0:T(8,128)(2,1)S(1)} %copy-done, bf16[1,128,1536]{2,1,0:T(8,128)(2,1)S(1)} %copy-done.1, f32[128]{0:T(128)S(1)} %get-tuple-element.41, f32[128]{0:T(128)S(1)} %broadcast_multiply_fusion.3, f32[128]{0:T(128)S(1)} %broadcast_select_fusion.1), kind=kOutput, calls=%fused_computation.46 | convolution fusion | flops 1209335808 | bytes 11798016 | tf_op jit(solution)/shard_map/dot_general | solution.py:572
  92.0 1.3 fusion.23
  93.3 67.3 %shard_map.104 = (f32[2,1536]{1,0:T(2,128)}, f32[32,1536]{1,0:T(8,128)}, bf16[128,1536]{1,0:T(8,128)(2,1)}) custom-call(f32[2,3,32]{2,1,0:T(4,128)} %pad_maximum_fusion.refs_0_, f32[2]{0:T(128)} %pad_maximum_fusion.3.refs_1_, bf16[128,1536]{1,0:T(8,128)(2,1)} %get-tuple-element.44.refs_2_, f32[128,1536]{1,0:T(8,128)} %get-tuple-element.43.refs_3_, ...), custom_call_target="tpu_custom_call" | custom-call | tf_op jit(solution)/shard_map/pallas_call | solution.py:277
  160.6 1.3 fusion.2
  161.9 5.3 %fusion.41 = (f32[128]{0:T(128)S(1)}, f32[128]{0:T(128)S(1)}, f32[128,1536]{1,0:T(8,128)S(1)}) fusion(f32[128]{0:T(128)S(1)} %get-tuple-element.41, f32[128]{0:T(128)S(1)} %broadcast_multiply_fusion.3, f32[128]{0:T(128)S(1)} %broadcast_select_fusion.1, bf16[1,128,1536]{2,1,0:T(8,128)(2,1)S(1)} %copy-done, bf16[1,128,1536]{2,1,0:T(8,128)(2,1)S(1)} %copy-done.1, ...), kind=kOutput, calls=%fused_computation.81 | convolution fusion | flops 1211301632 | bytes 11799040 | tf_op jit(solution)/shard_map/dot_general | solution.py:594
  168.2 17.6 %shard_map.105 = f32[1,128]{1,0:T(1,128)} custom-call(f32[1,128]{1,0:T(1,128)} %bitcast.87), custom_call_target="tpu_custom_call" | custom-call | tf_op jit(solution)/shard_map/pallas_call | solution.py:325
  185.8 1.3 reduce_sum.126
  187.8 1.1 fusion.42
  189.2 6.8 %fusion.28 = f32[128,3072]{1,0:T(8,128)S(1)} fusion(bf16[3072,1536]{1,0:T(8,128)(2,1)} %bitcast.79, f32[128,1536]{1,0:T(8,128)S(1)} %get-tuple-element.28, f32[128]{0:T(128)S(1)} %add_rsqrt_fusion, f32[128]{0:T(128)S(1)} %broadcast_multiply_fusion), kind=kOutput, calls=%fused_computation.44 | convolution fusion | flops 1208549376 | bytes 11797504 | tf_op jit(solution)/shard_map/dot_general | solution.py:572
  196.0 1.0 fusion.24.refs_2_
  196.9 61.9 %shard_map.106 = (f32[2,1536]{1,0:T(2,128)}, f32[32,1536]{1,0:T(8,128)}) custom-call(f32[2,3,32]{2,1,0:T(4,128)} %pad_maximum_fusion.refs_0_, f32[2]{0:T(128)} %pad_maximum_fusion.3.refs_1_, bf16[128,1536]{1,0:T(8,128)(2,1)} %fusion.24.refs_2_, f32[128,1536]{1,0:T(8,128)} %get-tuple-element.43.refs_3_, f32[128,128]{1,0:T(8,128)} %broadcast_in_dim.12.refs_4_, ...), custom_call_target="tpu_custom_call" | custom-call | tf_op jit(solution)/shard_map/pallas_call | solution.py:277
  258.8 1.3 dynamic-slice_add_fusion
  260.1 1.0 slice_add_fusion
  261.1 1.7 reshape.191
  264.6 21.8 %shard_map.107 = f32[8,128]{1,0:T(8,128)} custom-call(f32[2,16,2,8,128]{4,3,2,1,0:T(8,128)} %bitcast.81), custom_call_target="tpu_custom_call" | custom-call | tf_op jit(solution)/shard_map/pallas_call | solution.py:354
  286.4 0.8 reshape.195
  (40 shorter events, 8.6 us)
Async XLA Ops:
  0.6 84.4 %copy-start = (bf16[1,128,1536]{2,1,0:T(8,128)(2,1)S(1)}, bf16[1,128,1536]{2,1,0:T(8,128)(2,1)}, u32[]{:S(2)}) copy-start(bf16[1,128,1536]{2,1,0:T(8,128)(2,1)} %param.9) | copy-start | bytes 1179652
  0.6 84.4 %copy-start.1 = (bf16[1,128,1536]{2,1,0:T(8,128)(2,1)S(1)}, bf16[1,128,1536]{2,1,0:T(8,128)(2,1)}, u32[]{:S(2)}) copy-start(bf16[1,128,1536]{2,1,0:T(8,128)(2,1)} %param.8) | copy-start | bytes 1179652
  17.2 74.8 %copy-start.2 = (bf16[1,128,1536]{2,1,0:T(8,128)(2,1)S(1)}, bf16[1,128,1536]{2,1,0:T(8,128)(2,1)}, u32[]{:S(2)}) copy-start(bf16[1,128,1536]{2,1,0:T(8,128)(2,1)} %param.10) | copy-start | bytes 1179652
  187.8 72.3 %copy-start.3 = (f32[32,1536]{1,0:T(8,128)S(1)}, f32[32,1536]{1,0:T(8,128)}, u32[]{:S(2)}) copy-start(f32[32,1536]{1,0:T(8,128)} %get-tuple-element.9) | copy-start | bytes 589828

commit v6 on v5

--- a/solution.py
+++ b/solution.py
@@ -115,15 +115,51 @@
     )
 
 
-def sum_everywhere(src, b1, b2, b3, sems, join):
-    plane, column = flat_plane(), groups()[2]
-    me, z = plane[1], column[1]
-    b1[me] = src[me]
-    exchange(plane, lambda peer: src.at[peer], b1, sems.at[0])
-    b2[z] = join(b1, 32, 0)
-    exchange(column, lambda peer: b2.at[z], b2, sems.at[1])
-    b3[me] = join(b2, 16, 1)
-    exchange(plane, lambda peer: b3.at[me], b3, sems.at[2])
+def sum_everywhere(owners, src, b1, b2, b3, sems, join):
+    (count, me, where), column = flat_plane(), groups()[2]
+    z = column[1]
+
+    def copy(stage, source, landing, send, receive, peer):
+        return pltpu.make_async_remote_copy(
+            src_ref=source,
+            dst_ref=landing,
+            send_sem=sems.at[stage, 0, send],
+            recv_sem=sems.at[stage, 1, receive],
+            device_id=where(peer),
+            device_id_type=pl.DeviceIdType.MESH,
+        )
+
+    def for_owners(body):
+        def step(i, carry):
+            @pl.when(i != me)
+            def _():
+                body(i)
+
+            return carry
+
+        lax.fori_loop(0, owners, step, 0)
+
+    def for_peers(body):
+        def step(d, carry):
+            body(d, lax.rem(me + d, count))
+            return carry
+
+        lax.fori_loop(1, count, step, 0)
+
+    for_owners(lambda i: copy(0, src.at[i], b1.at[me], i, me, i).start())
+
+    @pl.when(me < owners)
+    def _():
+        b1[me] = src[me]
+        for_peers(lambda d, peer: copy(0, src.at[0], b1.at[peer], 0, peer, peer).wait_recv())
+        b2[z] = join(b1, 32, 0)
+        exchange(column, lambda peer: b2.at[z], b2, sems.at[1])
+        b3[me] = join(b2, 16, 1)
+        for_peers(lambda d, peer: copy(2, b3.at[me], b3.at[me], d, me, peer).start())
+        for_peers(lambda d, peer: copy(2, b3.at[me], b3.at[me], d, me, peer).wait_send())
+
+    for_owners(lambda i: copy(0, src.at[i], b1.at[me], i, me, i).wait_send())
+    for_owners(lambda i: copy(2, b3.at[i], b3.at[i], 0, i, i).wait_recv())
 
 
 def neighbours():
@@ -187,8 +223,6 @@
     first_halo = halo_copies(glu_ref, halo1, 0)
     for copy in first_halo:
         copy.start()
-    s1[...] = jnp.zeros(s1.shape, jnp.float32)
-    s2[...] = jnp.zeros(s2.shape, jnp.float32)
     for copy in first_halo:
         copy.wait()
     fill(glu_ref, halo1)
@@ -202,7 +236,7 @@
         s1[i, 1:2] = jnp.sum(live * apart * apart, axis=0, keepdims=True)
 
     each(moments)
-    sum_everywhere(s1, a1, a2, a3, sems1, lambda p, n, k: join_moments(p, n, sizes, k))
+    sum_everywhere(width // 128, s1, a1, a2, a3, sems1, lambda p, n, k: join_moments(p, n, sizes, k))
 
     def activate(i):
         found = a3[i]
@@ -218,7 +252,7 @@
         s2[i, 1:2] = jnp.sum(grad_pre, axis=0, keepdims=True)
 
     each(activate)
-    sum_everywhere(s2, c1, c2, c3, sems2, lambda p, n, k: add_up(p, n))
+    sum_everywhere(width // 128, s2, c1, c2, c3, sems2, lambda p, n, k: add_up(p, n))
 
     def backward(i):
         found = c3[i]
@@ -295,7 +329,7 @@
         + [pltpu.SemaphoreType.DMA((2, 4))],
         compiler_params=pltpu.CompilerParams(collective_id=number, has_side_effects=True),
     )(sizes, counts, glu, upstream, jnp.broadcast_to(live, (rows, 128)),
-      jnp.pad(kernel, ((0, 1), (0, 0))), gain[None], shift[None])
+      kernel, gain[None], shift[None])
 
 
 def group_sizes(ends, frame_rows):

time: 290 us -> 285 us (0.983)
    pallas_call x2, Pallas kernels: 129 us -> 125 us  [conv_step(): pl.pallas_call(body, out_shape=shapes, in_specs=[smem, smem] + [vmem] * 6...]
where the time goes in v6:
time: 285 us; the launch traced here: 284 us
  Pallas kernels  234 us (82%)
  matrix products  19 us (7%)
  other arithmetic  16.5 us (6%)
  local copies, waits for them, and re-layouts  10.7 us (4%)
  between operations  3.63 us (1%)
    pallas_call x2, Pallas kernels, conv_step(): pl.pallas_call(body, out_shape=shapes, in_specs=[smem, smem] + [vmem] * 6...  125 us
    pallas_call x1, Pallas kernels, gather(): pl.pallas_call(gather_kernel, out_shape=jax.ShapeDtypeStruct((16, 2, 2, s...  67.8 us
    pallas_call x1, Pallas kernels, scatter_taps(): pl.pallas_call(scatter_taps_kernel, out_shape=jax.ShapeDtypeStruct((8, 12...  22.6 us
    pallas_call x1, Pallas kernels, square_sum(): pl.pallas_call(square_sum_kernel, out_shape=jax.ShapeDtypeStruct((1, 128)...  17.9 us
    dot_general x2, matrix products, on_device(): lax.dot_general(normed.astype(jnp.bfloat16), weight_full, (((1,), (1,)),...  13.7 us

profile of v6, /device:TPU:1, one launch (start us, length us, event | category | flops | bytes accessed | tf_op | source)
XLA Modules:
  0.0 283.7 jit_solution(2119826623860244808)
XLA Ops:
  0.7 1.3 dynamic_slice.11
  2.7 1.3 reduce_sum.120
  5.3 1.4 fusion.26
  6.7 1.4 multiply_reduce_fusion.3
  11.0 1.3 broadcast_in_dim.13.refs_6_
  12.3 1.3 broadcast_in_dim.14.refs_7_
  15.6 67.8 %shard_map.103 = bf16[16,2,2,6,8,1536]{5,4,3,2,1,0:T(8,128)(2,1)} custom-call(bf16[6,8,1536]{2,1,0:T(8,128)(2,1)} %bitcast.82), custom_call_target="tpu_custom_call" | custom-call | tf_op jit(solution)/shard_map/pallas_call | solution.py:568
  83.5 6.9 %fusion.30 = f32[128,3072]{1,0:T(8,128)S(1)} fusion(bf16[3072,1536]{1,0:T(8,128)(2,1)} %bitcast.77, bf16[1,128,1536]{2,1,0:T(8,128)(2,1)S(1)} %copy-done, bf16[1,128,1536]{2,1,0:T(8,128)(2,1)S(1)} %copy-done.1, f32[128]{0:T(128)S(1)} %get-tuple-element.41, f32[128]{0:T(128)S(1)} %broadcast_multiply_fusion.3, f32[128]{0:T(128)S(1)} %broadcast_select_fusion.1), kind=kOutput, calls=%fused_computation.46 | convolution fusion | flops 1209335808 | bytes 11798016 | tf_op jit(solution)/shard_map/dot_general | solution.py:606
  90.4 1.3 fusion.23
  91.7 65.4 %shard_map.104 = (f32[2,1536]{1,0:T(2,128)}, f32[32,1536]{1,0:T(8,128)}, bf16[128,1536]{1,0:T(8,128)(2,1)}) custom-call(f32[2,3,32]{2,1,0:T(4,128)} %pad_maximum_fusion.refs_0_, f32[2]{0:T(128)} %pad_maximum_fusion.3.refs_1_, bf16[128,1536]{1,0:T(8,128)(2,1)} %get-tuple-element.44.refs_2_, f32[128,1536]{1,0:T(8,128)} %get-tuple-element.43.refs_3_, ...), custom_call_target="tpu_custom_call" | custom-call | tf_op jit(solution)/shard_map/pallas_call | solution.py:311
  157.1 1.3 fusion.2
  158.4 5.3 %fusion.41 = (f32[128]{0:T(128)S(1)}, f32[128]{0:T(128)S(1)}, f32[128,1536]{1,0:T(8,128)S(1)}) fusion(f32[128]{0:T(128)S(1)} %get-tuple-element.41, f32[128]{0:T(128)S(1)} %broadcast_multiply_fusion.3, f32[128]{0:T(128)S(1)} %broadcast_select_fusion.1, bf16[1,128,1536]{2,1,0:T(8,128)(2,1)S(1)} %copy-done, bf16[1,128,1536]{2,1,0:T(8,128)(2,1)S(1)} %copy-done.1, ...), kind=kOutput, calls=%fused_computation.81 | convolution fusion | flops 1211301632 | bytes 11799040 | tf_op jit(solution)/shard_map/dot_general | solution.py:628
  164.7 17.9 %shard_map.105 = f32[1,128]{1,0:T(1,128)} custom-call(f32[1,128]{1,0:T(1,128)} %bitcast.87), custom_call_target="tpu_custom_call" | custom-call | tf_op jit(solution)/shard_map/pallas_call | solution.py:359
  182.5 1.3 reduce_sum.126
  184.6 1.1 fusion.42
  185.9 6.8 %fusion.28 = f32[128,3072]{1,0:T(8,128)S(1)} fusion(bf16[3072,1536]{1,0:T(8,128)(2,1)} %bitcast.79, f32[128,1536]{1,0:T(8,128)S(1)} %get-tuple-element.28, f32[128]{0:T(128)S(1)} %add_rsqrt_fusion, f32[128]{0:T(128)S(1)} %broadcast_multiply_fusion), kind=kOutput, calls=%fused_computation.44 | convolution fusion | flops 1208549376 | bytes 11797504 | tf_op jit(solution)/shard_map/dot_general | solution.py:606
  192.7 1.0 fusion.24.refs_2_
  193.7 60.1 %shard_map.106 = (f32[2,1536]{1,0:T(2,128)}, f32[32,1536]{1,0:T(8,128)}) custom-call(f32[2,3,32]{2,1,0:T(4,128)} %pad_maximum_fusion.refs_0_, f32[2]{0:T(128)} %pad_maximum_fusion.3.refs_1_, bf16[128,1536]{1,0:T(8,128)(2,1)} %fusion.24.refs_2_, f32[128,1536]{1,0:T(8,128)} %get-tuple-element.43.refs_3_, f32[128,128]{1,0:T(8,128)} %broadcast_in_dim.12.refs_4_, ...), custom_call_target="tpu_custom_call" | custom-call | tf_op jit(solution)/shard_map/pallas_call | solution.py:311
  253.8 1.3 dynamic-slice_add_fusion
  255.1 1.0 slice_add_fusion
  256.1 1.7 reshape.191
  258.9 0.7 copy.35
  259.6 22.6 %shard_map.107 = f32[8,128]{1,0:T(8,128)} custom-call(f32[2,16,2,8,128]{4,3,2,1,0:T(8,128)} %bitcast.81), custom_call_target="tpu_custom_call" | custom-call | tf_op jit(solution)/shard_map/pallas_call | solution.py:388
  282.3 0.8 reshape.195
  (39 shorter events, 7.9 us)
Async XLA Ops:
  0.6 82.8 %copy-start = (bf16[1,128,1536]{2,1,0:T(8,128)(2,1)S(1)}, bf16[1,128,1536]{2,1,0:T(8,128)(2,1)}, u32[]{:S(2)}) copy-start(bf16[1,128,1536]{2,1,0:T(8,128)(2,1)} %param.9) | copy-start | bytes 1179652
  0.6 82.8 %copy-start.1 = (bf16[1,128,1536]{2,1,0:T(8,128)(2,1)S(1)}, bf16[1,128,1536]{2,1,0:T(8,128)(2,1)}, u32[]{:S(2)}) copy-start(bf16[1,128,1536]{2,1,0:T(8,128)(2,1)} %param.8) | copy-start | bytes 1179652
  15.6 74.8 %copy-start.2 = (bf16[1,128,1536]{2,1,0:T(8,128)(2,1)S(1)}, bf16[1,128,1536]{2,1,0:T(8,128)(2,1)}, u32[]{:S(2)}) copy-start(bf16[1,128,1536]{2,1,0:T(8,128)(2,1)} %param.10) | copy-start | bytes 1179652
  184.5 70.6 %copy-start.3 = (f32[32,1536]{1,0:T(8,128)S(1)}, f32[32,1536]{1,0:T(8,128)}, u32[]{:S(2)}) copy-start(f32[32,1536]{1,0:T(8,128)} %get-tuple-element.9) | copy-start | bytes 589828
